TPU v7x, 512 devices: a whole 4x4x16 slice. The times are simulated.
512 devices in a mesh: ctx: 64 (over x, z), head: 8 (over y, core).
Axes of the slice: x: 4, y: 4, z: 16, core: 2. Of those that a mesh axis runs over, the one named last changes fastest.
Arguments:
- queries: bfloat16 [12288, 6144], P(('ctx', 'head')), may hold values from -9 to 9
- noisy_token_keys: bfloat16 [12288, 1024], P(('ctx', 'head')), may hold values from -9 to 9
- noisy_token_values: bfloat16 [12288, 1024], P(('ctx', 'head')), may hold values from -6 to 6
- clean_token_keys: bfloat16 [4096, 1024], P(('ctx', 'head')), may hold values from -9 to 9
- clean_token_values: bfloat16 [4096, 1024], P(('ctx', 'head')), may hold values from -6 to 6
- output_gradient: bfloat16 [12288, 6144], P(('ctx', 'head')), may hold values from -6 to 6
- history_list: int32 [64, 64], replicated, may hold values from -1 to 1, as said below
Outputs:
- attn_out: bfloat16 [12288, 6144], P(('ctx', 'head'))
- grad_query: bfloat16 [12288, 6144], P(('ctx', 'head'))
- noisy_key_gradient: bfloat16 [12288, 1024], P(('ctx', 'head'))
- noisy_value_gradient: bfloat16 [12288, 1024], P(('ctx', 'head'))
- grad_key_clean: bfloat16 [4096, 1024], P(('ctx', 'head'))
- grad_value_clean: bfloat16 [4096, 1024], P(('ctx', 'head'))
Inputs may be any that keep to these rules, and one draw needn't show every extreme that they name: history_list[d, s] is -1 or a block number below 2; it is -1 unless floor(s / 2) < floor(d / 2); each row has at most 62 entries that are not -1, and some row has exactly 62.
All inputs are finite; a program needn't handle non-finite values.
Results may differ from a plain program's by a relative error of at most 0.018.
Values may be sent and summed in bfloat16 or wider, within the bound.
A program may use at most 64 MiB of HBM per device.

v0:
```python
import jax
import jax.numpy as jnp
from jax import lax
from jax.sharding import PartitionSpec as P

QUERY_HEADS = 48
KEY_VALUE_HEADS = 8
HEAD_SIZE = 128
BLK = 32


NEG_FILL = -1e30


def swapped(block, axis, bit):
    count = lax.axis_size(axis)
    route = []
    for low in range(count):
        high = low | 1 << bit
        if high != low and high < count:
            route += [(low, high), (high, low)]
    return lax.ppermute(block, axis, route)


def shards(
    queries,
    noisy_token_keys,
    noisy_token_values,
    clean_token_keys,
    clean_token_values,
    output_gradient,
    history_list,
):
    query_local, upstream_flat, key_fresh, value_fresh, key_stored, value_stored = (
        lax.all_to_all(queries, "head", split_axis=1, concat_axis=0, tiled=True),
        lax.all_to_all(output_gradient, "head", split_axis=1, concat_axis=0, tiled=True),
        lax.all_to_all(noisy_token_keys, "head", split_axis=1, concat_axis=0, tiled=True),
        lax.all_to_all(noisy_token_values, "head", split_axis=1, concat_axis=0, tiled=True),
        lax.all_to_all(clean_token_keys, "head", split_axis=1, concat_axis=0, tiled=True),
        lax.all_to_all(clean_token_values, "head", split_axis=1, concat_axis=0, tiled=True),
    )
    ctx_count = lax.axis_size("ctx")
    count_of_heads = lax.axis_size("head")
    position = lax.axis_index("ctx")
    key_value_groups = KEY_VALUE_HEADS // count_of_heads
    heads_per_group = QUERY_HEADS // KEY_VALUE_HEADS
    logit_scale = HEAD_SIZE ** (-0.5)
    query_matrix_rows = query_local.shape[0]
    clean_rows = key_stored.shape[0]
    block_count = clean_rows // BLK
    row_width = key_value_groups * HEAD_SIZE
    query_heads = query_local.reshape(
        query_matrix_rows, key_value_groups, heads_per_group, HEAD_SIZE
    )
    incoming_gradient = upstream_flat.reshape(
        query_matrix_rows, key_value_groups, heads_per_group, HEAD_SIZE
    )
    requested = lax.dynamic_index_in_dim(history_list, position, 0, keepdims=False)
    wanted_from_me = lax.dynamic_index_in_dim(history_list, position, 1, keepdims=False)
    key_partner, value_partner = swapped((key_fresh, value_fresh), "ctx", 0)
    keys_in_span = jnp.concatenate([key_fresh, key_partner], 0).reshape(
        2 * query_matrix_rows, key_value_groups, HEAD_SIZE
    )
    values_in_span = jnp.concatenate([value_fresh, value_partner], 0).reshape(
        2 * query_matrix_rows, key_value_groups, HEAD_SIZE
    )
    span_live = jnp.ones((2 * query_matrix_rows,), jnp.bool_)
    which_block = jnp.maximum(wanted_from_me, 0)
    keep_slot = (wanted_from_me >= 0)[:, None, None]
    send_keys = jnp.where(
        keep_slot,
        key_stored.reshape(block_count, BLK, row_width)[which_block],
        jnp.zeros((), jnp.bfloat16),
    )
    send_values = jnp.where(
        keep_slot,
        value_stored.reshape(block_count, BLK, row_width)[which_block],
        jnp.zeros((), jnp.bfloat16),
    )
    key_history, value_history = (
        lax.all_to_all(send_keys, "ctx", split_axis=0, concat_axis=0, tiled=True),
        lax.all_to_all(send_values, "ctx", split_axis=0, concat_axis=0, tiled=True),
    )
    live_slots = requested >= 0
    slot_group = min(ctx_count, max(1, 512 // BLK))
    turns = ctx_count // slot_group

    def clean_tile(turn):
        first_slot = turn * slot_group
        tile_keys = lax.dynamic_slice_in_dim(key_history, first_slot, slot_group, 0).reshape(
            slot_group * BLK, key_value_groups, HEAD_SIZE
        )
        tile_values = lax.dynamic_slice_in_dim(value_history, first_slot, slot_group, 0).reshape(
            slot_group * BLK, key_value_groups, HEAD_SIZE
        )
        tile_live = jnp.repeat(lax.dynamic_slice_in_dim(live_slots, first_slot, slot_group, 0), BLK)
        return (tile_keys, tile_values, tile_live)

    def tile_scores(tile_keys, tile_live):
        scores = (
            jnp.einsum("qgrd,kgd->gqrk", query_heads, tile_keys, preferred_element_type=jnp.float32)
            * logit_scale
        )
        return jnp.where(tile_live, scores, NEG_FILL)

    first_scores = tile_scores(keys_in_span, span_live)
    running_max = jnp.max(first_scores, -1)
    denominator = jnp.sum(jnp.exp(first_scores - running_max[..., None]), -1)

    def statistics_step(turn, state):
        old_max, old_sum = state
        tile_keys, tile_values, tile_live = clean_tile(turn)
        scores = tile_scores(tile_keys, tile_live)
        new_max = jnp.maximum(old_max, jnp.max(scores, -1))
        new_sum = old_sum * jnp.exp(old_max - new_max) + jnp.sum(
            jnp.exp(scores - new_max[..., None]), -1
        )
        return (new_max, new_sum)

    running_max, denominator = lax.fori_loop(0, turns, statistics_step, (running_max, denominator))
    log_total = (running_max + jnp.log(denominator))[..., None]

    def output_tile(tile_keys, tile_values, tile_live):
        softmax_weights = jnp.exp(tile_scores(tile_keys, tile_live) - log_total).astype(
            jnp.bfloat16
        )
        return jnp.einsum(
            "gqrk,kgd->qgrd", softmax_weights, tile_values, preferred_element_type=jnp.float32
        )

    def output_step(turn, partial_sum):
        return partial_sum + output_tile(*clean_tile(turn))

    attended_sum = lax.fori_loop(
        0, turns, output_step, output_tile(keys_in_span, values_in_span, span_live)
    )
    attended = attended_sum.astype(jnp.bfloat16)
    row_dot = jnp.einsum(
        "qgrd,qgrd->gqr", incoming_gradient, attended, preferred_element_type=jnp.float32
    )[..., None]

    def gradient_tile(tile_keys, tile_values, tile_live):
        probabilities = jnp.exp(tile_scores(tile_keys, tile_live) - log_total)
        softmax_weights = probabilities.astype(jnp.bfloat16)
        dprobs = jnp.einsum(
            "qgrd,kgd->gqrk", incoming_gradient, tile_values, preferred_element_type=jnp.float32
        )
        score_gradient = (probabilities * (dprobs - row_dot)).astype(jnp.bfloat16)
        query_part = jnp.einsum(
            "gqrk,kgd->qgrd", score_gradient, tile_keys, preferred_element_type=jnp.float32
        )
        key_part = (
            jnp.einsum(
                "xtlv,txlh->vxh", score_gradient, query_heads, preferred_element_type=jnp.float32
            )
            * logit_scale
        )
        value_part = jnp.einsum(
            "xtlv,txlh->vxh", softmax_weights, incoming_gradient, preferred_element_type=jnp.float32
        )
        return (query_part, key_part.reshape(-1, row_width), value_part.reshape(-1, row_width))

    query_sum, span_key_grad, span_value_grad = gradient_tile(
        keys_in_span, values_in_span, span_live
    )
    empty_grads = jnp.zeros((ctx_count, BLK, row_width), jnp.float32)

    def gradient_step(turn, state):
        query_part_sum, slot_keys, slot_values = state
        query_part, key_part, value_part = gradient_tile(*clean_tile(turn))
        first_slot = turn * slot_group
        slot_keys = lax.dynamic_update_slice_in_dim(
            slot_keys, key_part.reshape(slot_group, BLK, row_width), first_slot, 0
        )
        slot_values = lax.dynamic_update_slice_in_dim(
            slot_values, value_part.reshape(slot_group, BLK, row_width), first_slot, 0
        )
        return (query_part_sum + query_part, slot_keys, slot_values)

    query_sum, slot_key_grads, slot_value_grads = lax.fori_loop(
        0, turns, gradient_step, (query_sum, empty_grads, empty_grads)
    )
    query_grad = (query_sum * logit_scale).astype(jnp.bfloat16)
    partner_key_grad, partner_value_grad = swapped(
        (span_key_grad[query_matrix_rows:], span_value_grad[query_matrix_rows:]), "ctx", 0
    )
    fresh_key_grad = (span_key_grad[:query_matrix_rows] + partner_key_grad).astype(jnp.bfloat16)
    fresh_value_grad = (span_value_grad[:query_matrix_rows] + partner_value_grad).astype(
        jnp.bfloat16
    )
    returned_keys, returned_values = (
        lax.all_to_all(slot_key_grads, "ctx", split_axis=0, concat_axis=0, tiled=True),
        lax.all_to_all(slot_value_grads, "ctx", split_axis=0, concat_axis=0, tiled=True),
    )
    owner_table = (
        wanted_from_me[:, None] == jnp.arange(block_count, dtype=jnp.int32)[None, :]
    ).astype(jnp.float32)
    stored_key_grad = (
        jnp.einsum("rb,rtc->btc", owner_table, returned_keys, precision=lax.Precision.HIGHEST)
        .reshape(clean_rows, row_width)
        .astype(jnp.bfloat16)
    )
    stored_value_grad = (
        jnp.einsum("rb,rtc->btc", owner_table, returned_values, precision=lax.Precision.HIGHEST)
        .reshape(clean_rows, row_width)
        .astype(jnp.bfloat16)
    )
    results = (
        lax.all_to_all(
            attended.reshape(query_matrix_rows, key_value_groups * heads_per_group * HEAD_SIZE),
            "head",
            split_axis=0,
            concat_axis=1,
            tiled=True,
        ),
        lax.all_to_all(
            query_grad.reshape(query_matrix_rows, key_value_groups * heads_per_group * HEAD_SIZE),
            "head",
            split_axis=0,
            concat_axis=1,
            tiled=True,
        ),
        lax.all_to_all(fresh_key_grad, "head", split_axis=0, concat_axis=1, tiled=True),
        lax.all_to_all(fresh_value_grad, "head", split_axis=0, concat_axis=1, tiled=True),
        lax.all_to_all(stored_key_grad, "head", split_axis=0, concat_axis=1, tiled=True),
        lax.all_to_all(stored_value_grad, "head", split_axis=0, concat_axis=1, tiled=True),
    )
    return tuple(results)


def solution(mesh):
    placed = (
        P(("ctx", "head"), None),
        P(("ctx", "head"), None),
        P(("ctx", "head"), None),
        P(("ctx", "head"), None),
        P(("ctx", "head"), None),
        P(("ctx", "head"), None),
        P(),
    )
    return jax.shard_map(
        shards,
        mesh=mesh,
        in_specs=placed,
        out_specs=(
            P(("ctx", "head"), None),
            P(("ctx", "head"), None),
            P(("ctx", "head"), None),
            P(("ctx", "head"), None),
            P(("ctx", "head"), None),
            P(("ctx", "head"), None),
        ),
        check_vma=False,
    )
```

profile of v0, /device:TPU:1, one launch (start us, length us, event | category | flops | bytes accessed | tf_op | source)
XLA Modules:
  0.0 407.8 jit_solution(4642079409190088269)
XLA Ops:
  0.6 14.9 %all_to_all.230 = bf16[8,8,128]{2,0,1:T(8,128)(2,1)S(1)} all-to-all(bf16[8,8,128]{2,0,1:T(8,128)(2,1)} %bitcast.360), channel_id=1, replica_groups=mesh['ctx'=64,'head'=8] {'head'}, dimensions={1} | all-to-all | bytes 32768 | tf_op jit(solution)/shard_map/all_to_all | solution.py:39
  15.5 4.0 all-to-all-start.5
  20.1 4.0 all-to-all-done.5
  24.1 4.0 all-to-all-start.1
  29.5 3.4 all-to-all-done.1
  32.9 4.6 %all-to-all-start = ((bf16[24,8,128]{2,0,1:T(8,128)(2,1)}), bf16[24,8,128]{2,0,1:T(8,128)(2,1)}, u32[]{:S(2)}, u32[]{:S(2)}) async-start(bf16[24,8,128]{2,0,1:T(8,128)(2,1)} %copy_bitcast_fusion.5), calls=%async_computation | async-start | bytes 98304 | tf_op jit(solution)/shard_map/all_to_all | solution.py:38
  37.5 1.7 copy.119
  40.1 2.3 all-to-all-done
  42.4 4.1 %all-to-all-start.2 = ((bf16[24,8,768]{2,0,1:T(8,128)(2,1)}), bf16[24,8,768]{2,0,1:T(8,128)(2,1)S(1)}, u32[]{:S(2)}, u32[]{:S(2)}) async-start(bf16[24,8,768]{2,0,1:T(8,128)(2,1)} %bitcast.259), calls=%async_computation.2 | async-start | bytes 589824 | tf_op jit(solution)/shard_map/all_to_all | solution.py:35
  46.5 1.7 copy.118
  49.5 3.8 all-to-all-done.2
  53.3 4.4 %all-to-all-start.8 = ((bf16[24,8,768]{2,0,1:T(8,128)(2,1)}), bf16[24,8,768]{2,0,1:T(8,128)(2,1)S(1)}, u32[]{:S(2)}, u32[]{:S(2)}) async-start(bf16[24,8,768]{2,0,1:T(8,128)(2,1)} %bitcast.258), calls=%async_computation.8 | async-start | bytes 589824 | tf_op jit(solution)/shard_map/all_to_all | solution.py:36
  58.8 5.7 %all-to-all-done.8 = bf16[24,8,768]{2,0,1:T(8,128)(2,1)S(1)} async-done(((bf16[24,8,768]{2,0,1:T(8,128)(2,1)}), bf16[24,8,768]{2,0,1:T(8,128)(2,1)S(1)}, u32[]{:S(2)}, u32[]{:S(2)}) %all-to-all-start.8) | async-done | bytes 294944 | tf_op jit(solution)/shard_map/all_to_all | solution.py:36
  64.5 14.2 %all-to-all-start.4 = ((bf16[64,32,128]{2,1,0:T(8,128)(2,1)}), bf16[64,32,128]{2,1,0:T(8,128)(2,1)S(1)}, u32[]{:S(2)}, u32[]{:S(2)}) async-start(bf16[64,32,128]{2,1,0:T(8,128)(2,1)} %get-tuple-element.572), calls=%async_computation.4 | async-start | bytes 1048576 | tf_op jit(solution)/shard_map/all_to_all | solution.py:81
  78.7 2.9 collective-permute-start.1
  82.8 2.4 collective-permute-start
  88.1 12.7 %collective-permute-done.1 = bf16[192,128]{1,0:T(8,128)(2,1)S(1)} collective-permute-done((bf16[192,128]{1,0:T(8,128)(2,1)S(1)}, bf16[192,128]{1,0:T(8,128)(2,1)S(1)}, u32[]{:S(2)}, u32[]{:S(2)}) %collective-permute-start.1) | collective-permute-done | bytes 49184 | tf_op jit(solution)/shard_map/ppermute | solution.py:22
  103.6 4.5 %all-to-all-done.4 = bf16[64,32,128]{2,1,0:T(8,128)(2,1)S(1)} async-done(((bf16[64,32,128]{2,1,0:T(8,128)(2,1)}), bf16[64,32,128]{2,1,0:T(8,128)(2,1)S(1)}, u32[]{:S(2)}, u32[]{:S(2)}) %all-to-all-start.4) | async-done | bytes 524320 | tf_op jit(solution)/shard_map/all_to_all | solution.py:81
  108.2 12.1 %all-to-all-start.6 = ((bf16[64,32,128]{2,1,0:T(8,128)(2,1)}), bf16[64,32,128]{2,1,0:T(8,128)(2,1)S(1)}, u32[]{:S(2)}, u32[]{:S(2)}) async-start(bf16[64,32,128]{2,1,0:T(8,128)(2,1)} %get-tuple-element.571), calls=%async_computation.6 | async-start | bytes 1048576 | tf_op jit(solution)/shard_map/all_to_all | solution.py:82
  120.2 23.3 %while.45 = (s32[]{:T(128)}, f32[1,192,6]{1,2,0:T(8,128)}, f32[1,192,6]{1,2,0:T(8,128)}, pred[64]{0:T(512)(128)(4,1)}, bf16[64,32,128]{2,1,0:T(8,128)(2,1)S(1)},...) while((s32[]{:T(128)}, f32[1,192,6]{1,2,0:T(8,128)}, ...), condition=%wide.region_5.6_spmd, body=%wide.region_2.5_spmd.sunk | while | flops 155126016 | bytes 5526843 | solution.py:120
  146.9 2.9 collective-permute-start.3
  149.8 2.1 convolution_bitcast_fusion.3
  151.9 24.9 %while.46 = (s32[]{:T(128)}, f32[192,1,6,128]{3,0,2,1:T(8,128)}, bf16[64,32,128]{2,1,0:T(8,128)(2,1)S(1)}, pred[64]{0:T(512)(128)(4,1)}, bf16[64,32,128]{2,1,0:T...) while((s32[]{:T(128)}, f32[192,1,6,128]{3,0,2,1:T(8,128)}, ...), condition=%wide.region_7.8_spmd, body=%wide.region_6.7_spmd.sunk | while | flops 304496640 | bytes 2267859 | solution.py:134
  155.2 2.9 fusion.100
  161.4 2.9 fusion.100
  167.6 2.9 fusion.100
  173.9 2.9 fusion.100
  176.8 2.1 bitcast_convert_fusion
  183.5 2.5 collective-permute-start.2
  188.7 28.5 %while.47 = (s32[]{:T(128)}, f32[192,1,6,128]{3,0,2,1:T(8,128)S(1)}, f32[64,32,128]{2,1,0:T(8,128)}, f32[64,32,128]{2,1,0:T(8,128)}, bf16[64,32,128]{2,1,0:T(8,1...) while((s32[]{:T(128)}, ...), condition=%wide.region_9.10_spmd, body=%wide.region_8.9_spmd.sunk | while | flops 761085952 | bytes 20857168 | solution.py:180
  191.2 1.8 fusion.112
  198.3 1.8 fusion.112
  205.4 1.8 fusion.112
  212.6 1.8 fusion.112
  218.9 5.7 %all-to-all-start.11 = ((bf16[8,24,128]{2,1,0:T(8,128)(2,1)}), bf16[8,24,128]{2,1,0:T(8,128)(2,1)S(1)}, u32[]{:S(2)}, u32[]{:S(2)}) async-start(bf16[8,24,128]{2,1,0:T(8,128)(2,1)} %bitcast.89), calls=%async_computation.11 | async-start | bytes 98304 | tf_op jit(solution)/shard_map/all_to_all | solution.py:224
  226.2 3.2 all-to-all-done.11
  229.4 4.0 all-to-all-start.10
  234.7 3.5 all-to-all-done.10
  238.2 4.1 %all-to-all-start.9 = ((bf16[8,24,768]{2,1,0:T(8,128)(2,1)}), bf16[8,24,768]{2,1,0:T(8,128)(2,1)S(1)}, u32[]{:S(2)}, u32[]{:S(2)}) async-start(bf16[8,24,768]{2,1,0:T(8,128)(2,1)} %all_to_all.194), calls=%async_computation.9 | async-start | bytes 589824 | tf_op jit(solution)/shard_map/all_to_all | solution.py:216
  242.9 6.2 %all-to-all-done.9 = bf16[8,24,768]{2,1,0:T(8,128)(2,1)S(1)} async-done(((bf16[8,24,768]{2,1,0:T(8,128)(2,1)}), bf16[8,24,768]{2,1,0:T(8,128)(2,1)S(1)}, u32[]{:S(2)}, u32[]{:S(2)}) %all-to-all-start.9) | async-done | bytes 294944 | tf_op jit(solution)/shard_map/all_to_all | solution.py:216
  249.1 10.7 %all_to_all.231 = bf16[8,24,768]{2,1,0:T(8,128)(2,1)S(1)} all-to-all(bf16[8,24,768]{2,1,0:T(8,128)(2,1)S(1)} %all_to_all.187), channel_id=1, replica_groups=mesh['ctx'=64,'head'=8] {'head'}, dimensions={0} | all-to-all | bytes 589824 | tf_op jit(solution)/shard_map/all_to_all | solution.py:209
  259.8 65.3 %all_to_all.232 = f32[64,32,128]{2,1,0:T(8,128)S(1)} all-to-all(f32[64,32,128]{2,1,0:T(8,128)} %get-tuple-element.430), channel_id=1, replica_groups=mesh['ctx'=64,'head'=8] {'ctx'}, dimensions={0} | all-to-all | bytes 2097152 | tf_op jit(solution)/shard_map/all_to_all | solution.py:192
  325.1 10.1 %all-to-all-start.14 = ((f32[64,32,128]{2,1,0:T(8,128)}), f32[64,32,128]{2,1,0:T(8,128)S(1)}, u32[]{:S(2)}, u32[]{:S(2)}) async-start(f32[64,32,128]{2,1,0:T(8,128)} %get-tuple-element.431), calls=%async_computation.14 | async-start | bytes 2097152 | tf_op jit(solution)/shard_map/all_to_all | solution.py:193
  337.5 48.1 %all-to-all-done.14 = f32[64,32,128]{2,1,0:T(8,128)S(1)} async-done(((f32[64,32,128]{2,1,0:T(8,128)}), f32[64,32,128]{2,1,0:T(8,128)S(1)}, u32[]{:S(2)}, u32[]{:S(2)}) %all-to-all-start.14) | async-done | bytes 1048608 | tf_op jit(solution)/shard_map/all_to_all | solution.py:193
  385.6 7.7 %all-to-all-start.13 = ((bf16[8,8,128]{2,1,0:T(8,128)(2,1)}), bf16[8,8,128]{2,1,0:T(8,128)(2,1)S(1)}, u32[]{:S(2)}, u32[]{:S(2)}) async-start(bf16[8,8,128]{2,1,0:T(8,128)(2,1)} %bitcast.92), calls=%async_computation.13 | async-start | bytes 32768 | tf_op jit(solution)/shard_map/all_to_all | solution.py:225
  395.0 3.0 all-to-all-done.13
  398.0 3.9 all-to-all-start.15
  404.0 2.6 all-to-all-done.15
  (231 shorter events, 92.6 us)
Async XLA Ops:
  0.6 18.8 %copy-start = (bf16[24,1024]{1,0:T(8,128)(2,1)S(1)}, bf16[24,1024]{1,0:T(8,128)(2,1)}, u32[]{:S(2)}) copy-start(bf16[24,1024]{1,0:T(8,128)(2,1)} %param.14) | copy-start | bytes 147460
  15.5 8.6 %all-to-all-start.5 = ((bf16[8,8,128]{2,0,1:T(8,128)(2,1)}), bf16[8,8,128]{2,0,1:T(8,128)(2,1)S(1)}, u32[]{:S(2)}, u32[]{:S(2)}) async-start(bf16[8,8,128]{2,0,1:T(8,128)(2,1)} %bitcast.361), calls=%async_computation.5 | async-start | bytes 32768 | tf_op jit(solution)/shard_map/all_to_all | solution.py:40
  24.1 8.8 %all-to-all-start.1 = ((bf16[24,8,128]{2,0,1:T(8,128)(2,1)}), bf16[24,8,128]{2,0,1:T(8,128)(2,1)S(1)}, u32[]{:S(2)}, u32[]{:S(2)}) async-start(bf16[24,8,128]{2,0,1:T(8,128)(2,1)} %copy_bitcast_fusion.4), calls=%async_computation.1 | async-start | bytes 98304 | tf_op jit(solution)/shard_map/all_to_all | solution.py:37
  32.9 67.9 %copy-start.9 = (bf16[24,8,128]{2,0,1:T(8,128)(2,1)}, bf16[24,8,128]{2,0,1:T(8,128)(2,1)S(1)}, u32[]{:S(2)}) copy-start(bf16[24,8,128]{2,0,1:T(8,128)(2,1)S(1)} %all-to-all-done.1) | copy-start | bytes 147460
  32.9 9.5 %all-to-all-start = ((bf16[24,8,128]{2,0,1:T(8,128)(2,1)}), bf16[24,8,128]{2,0,1:T(8,128)(2,1)}, u32[]{:S(2)}, u32[]{:S(2)}) async-start(bf16[24,8,128]{2,0,1:T(8,128)(2,1)} %copy_bitcast_fusion.5), calls=%async_computation | async-start | bytes 98304 | tf_op jit(solution)/shard_map/all_to_all | solution.py:38
  40.1 8.1 %copy-start.21 = (s32[64]{0:T(128)}, s32[64]{0:T(128)S(1)}, u32[]{:S(2)}) copy-start(s32[64]{0:T(128)S(1)} %get-tuple-element.511) | copy-start | bytes 772
  42.4 10.9 %all-to-all-start.2 = ((bf16[24,8,768]{2,0,1:T(8,128)(2,1)}), bf16[24,8,768]{2,0,1:T(8,128)(2,1)S(1)}, u32[]{:S(2)}, u32[]{:S(2)}) async-start(bf16[24,8,768]{2,0,1:T(8,128)(2,1)} %bitcast.259), calls=%async_computation.2 | async-start | bytes 589824 | tf_op jit(solution)/shard_map/all_to_all | solution.py:35
  53.3 11.2 %all-to-all-start.8 = ((bf16[24,8,768]{2,0,1:T(8,128)(2,1)}), bf16[24,8,768]{2,0,1:T(8,128)(2,1)S(1)}, u32[]{:S(2)}, u32[]{:S(2)}) async-start(bf16[24,8,768]{2,0,1:T(8,128)(2,1)} %bitcast.258), calls=%async_computation.8 | async-start | bytes 589824 | tf_op jit(solution)/shard_map/all_to_all | solution.py:36
  64.5 43.7 %all-to-all-start.4 = ((bf16[64,32,128]{2,1,0:T(8,128)(2,1)}), bf16[64,32,128]{2,1,0:T(8,128)(2,1)S(1)}, u32[]{:S(2)}, u32[]{:S(2)}) async-start(bf16[64,32,128]{2,1,0:T(8,128)(2,1)} %get-tuple-element.572), calls=%async_computation.4 | async-start | bytes 1048576 | tf_op jit(solution)/shard_map/all_to_all | solution.py:81
  78.7 22.1 %collective-permute-start.1 = (bf16[192,128]{1,0:T(8,128)(2,1)S(1)}, bf16[192,128]{1,0:T(8,128)(2,1)S(1)}, u32[]{:S(2)}, u32[]{:S(2)}) collective-permute-start(bf16[192,128]{1,0:T(8,128)(2,1)S(1)} %bitcast.348), channel_id=1, source_target_pairs={{0,8},{8,0},{16,24},{24,16},{32,40},{40,32},{48,56},{56,48},{64,72... | collective-permute-start | bytes 147464 | tf_op jit(solution)/shard_map/ppermute | solution.py:22
  82.8 67.0 %collective-permute-start = (bf16[192,128]{1,0:T(8,128)(2,1)}, bf16[192,128]{1,0:T(8,128)(2,1)}, u32[]{:S(2)}, u32[]{:S(2)}) collective-permute-start(bf16[192,128]{1,0:T(8,128)(2,1)} %bitcast.40), channel_id=1, source_target_pairs={{0,8},{8,0},{16,24},{24,16},{32,40},{40,32},{48,56},{56,48},{64,72... | collective-permute-start | bytes 147464 | tf_op jit(solution)/shard_map/ppermute | solution.py:22
  100.8 7.4 %copy-start.14 = (bf16[192,128]{1,0:T(8,128)(2,1)}, bf16[192,128]{1,0:T(8,128)(2,1)S(1)}, u32[]{:S(2)}) copy-start(bf16[192,128]{1,0:T(8,128)(2,1)S(1)} %collective-permute-done.1) | copy-start | bytes 147460
  102.3 5.8 %copy-start.4 = (f32[192,6]{0,1:T(8,128)}, f32[192,6]{0,1:T(8,128)S(1)}, u32[]{:S(2)}) copy-start(f32[192,6]{0,1:T(8,128)S(1)} %get-tuple-element.573) | copy-start | bytes 13828
  108.2 43.8 %all-to-all-start.6 = ((bf16[64,32,128]{2,1,0:T(8,128)(2,1)}), bf16[64,32,128]{2,1,0:T(8,128)(2,1)S(1)}, u32[]{:S(2)}, u32[]{:S(2)}) async-start(bf16[64,32,128]{2,1,0:T(8,128)(2,1)} %get-tuple-element.571), calls=%async_computation.6 | async-start | bytes 1048576 | tf_op jit(solution)/shard_map/all_to_all | solution.py:82
  122.8 1.2 copy-start.18
  122.9 2.0 copy-start.11
  128.7 1.2 copy-start.18
  128.7 2.0 copy-start.11
  134.5 1.2 copy-start.18
  134.5 2.0 copy-start.11
  140.3 2.0 copy-start.11
  144.8 5.0 %copy-start.17 = (f32[192,6]{0,1:T(8,128)}, f32[192,6]{0,1:T(8,128)S(1)}, u32[]{:S(2)}) copy-start(f32[192,6]{0,1:T(8,128)S(1)} %get-tuple-element.570) | copy-start | bytes 13828
  146.9 70.4 %collective-permute-start.3 = (f32[192,128]{1,0:T(8,128)}, f32[192,128]{1,0:T(8,128)}, u32[]{:S(2)}, u32[]{:S(2)}) collective-permute-start(f32[192,128]{1,0:T(8,128)} %slice_bitcast_fusion), channel_id=1, source_target_pairs={{0,8},{8,0},{16,24},{24,16},{32,40},{40,32},{48,56},{56,48},{64,72... | collective-permute-start | bytes 294920 | tf_op jit(solution)/shard_map/ppermute | solution.py:22
  176.8 6.7 %copy-start.3 = (bf16[64,32,128]{2,1,0:T(8,128)(2,1)}, bf16[64,32,128]{2,1,0:T(8,128)(2,1)S(1)}, u32[]{:S(2)}) copy-start(bf16[64,32,128]{2,1,0:T(8,128)(2,1)S(1)} %get-tuple-element.861) | copy-start | bytes 1572868
  181.5 1.4 copy-start.6
  181.5 4.5 %copy-start.10 = (bf16[24,8,128]{2,0,1:T(8,128)(2,1)S(1)}, bf16[24,8,128]{2,0,1:T(8,128)(2,1)}, u32[]{:S(2)}) copy-start(bf16[24,8,128]{2,0,1:T(8,128)(2,1)} %copy-done.9) | copy-start | bytes 147460
  181.5 4.5 %copy-start.15 = (bf16[192,128]{1,0:T(8,128)(2,1)S(1)}, bf16[192,128]{1,0:T(8,128)(2,1)}, u32[]{:S(2)}) copy-start(bf16[192,128]{1,0:T(8,128)(2,1)} %copy-done.14) | copy-start | bytes 147460
  182.9 5.7 %copy-start.19 = (f32[192,6]{0,1:T(8,128)S(1)}, f32[192,6]{0,1:T(8,128)}, u32[]{:S(2)}) copy-start(f32[192,6]{0,1:T(8,128)} %copy.88) | copy-start | bytes 13828
  182.9 5.7 %copy-start.20 = (f32[1,192,6,1]{1,2,3,0:T(8,128)S(1)}, f32[1,192,6,1]{1,2,3,0:T(8,128)}, u32[]{:S(2)}) copy-start(f32[1,192,6,1]{1,2,3,0:T(8,128)} %get-tuple-element.878) | copy-start | bytes 13828
  183.0 5.7 %copy-start.23 = (pred[64]{0:T(512)(128)(4,1)S(1)}, pred[64]{0:T(512)(128)(4,1)}, u32[]{:S(2)}) copy-start(pred[64]{0:T(512)(128)(4,1)} %get-tuple-element.880) | copy-start | bytes 196
  183.4 5.3 %copy-start.16 = (f32[384,1,128]{2,0,1:T(8,128)}, f32[384,1,128]{2,0,1:T(8,128)S(1)}, u32[]{:S(2)}) copy-start(f32[384,1,128]{2,0,1:T(8,128)S(1)} %fusion.37) | copy-start | bytes 589828
  183.5 41.1 %collective-permute-start.2 = (f32[192,128]{1,0:T(8,128)S(1)}, f32[192,128]{1,0:T(8,128)}, u32[]{:S(2)}, u32[]{:S(2)}) collective-permute-start(f32[192,128]{1,0:T(8,128)S(1)} %slice_bitcast_fusion.2), channel_id=1, source_target_pairs={{0,8},{8,0},{16,24},{24,16},{32,40},{40,32},{48,56},{56,48},{64,72... | collective-permute-start | bytes 294920 | tf_op jit(solution)/shard_map/ppermute | solution.py:22
  191.1 2.3 copy-start.13
  194.3 1.5 copy-start.2
  198.3 2.3 copy-start.13
  201.5 1.5 copy-start.2
  205.4 2.3 copy-start.13
  208.6 1.5 copy-start.2
  212.6 2.3 copy-start.13
  215.7 1.5 copy-start.2
  217.2 25.0 %copy-start.7 = (bf16[192,1,6,128]{3,0,2,1:T(8,128)(2,1)S(1)}, bf16[192,1,6,128]{3,0,2,1:T(8,128)(2,1)}, u32[]{:S(2)}) copy-start(bf16[192,1,6,128]{3,0,2,1:T(8,128)(2,1)} %get-tuple-element.562) | copy-start | bytes 884740
  218.9 10.5 %all-to-all-start.11 = ((bf16[8,24,128]{2,1,0:T(8,128)(2,1)}), bf16[8,24,128]{2,1,0:T(8,128)(2,1)S(1)}, u32[]{:S(2)}, u32[]{:S(2)}) async-start(bf16[8,24,128]{2,1,0:T(8,128)(2,1)} %bitcast.89), calls=%async_computation.11 | async-start | bytes 98304 | tf_op jit(solution)/shard_map/all_to_all | solution.py:224
  229.4 8.8 %all-to-all-start.10 = ((bf16[8,24,128]{2,1,0:T(8,128)(2,1)}), bf16[8,24,128]{2,1,0:T(8,128)(2,1)S(1)}, u32[]{:S(2)}, u32[]{:S(2)}) async-start(bf16[8,24,128]{2,1,0:T(8,128)(2,1)} %bitcast.78), calls=%async_computation.10 | async-start | bytes 98304 | tf_op jit(solution)/shard_map/all_to_all | solution.py:223
  238.2 10.9 %all-to-all-start.9 = ((bf16[8,24,768]{2,1,0:T(8,128)(2,1)}), bf16[8,24,768]{2,1,0:T(8,128)(2,1)S(1)}, u32[]{:S(2)}, u32[]{:S(2)}) async-start(bf16[8,24,768]{2,1,0:T(8,128)(2,1)} %all_to_all.194), calls=%async_computation.9 | async-start | bytes 589824 | tf_op jit(solution)/shard_map/all_to_all | solution.py:216
  242.9 93.0 %copy-start.22 = (s32[64]{0:T(128)S(1)}, s32[64]{0:T(128)}, u32[]{:S(2)}) copy-start(s32[64]{0:T(128)} %copy-done.21) | copy-start | bytes 772
  325.1 60.5 %all-to-all-start.14 = ((f32[64,32,128]{2,1,0:T(8,128)}), f32[64,32,128]{2,1,0:T(8,128)S(1)}, u32[]{:S(2)}, u32[]{:S(2)}) async-start(f32[64,32,128]{2,1,0:T(8,128)} %get-tuple-element.431), calls=%async_computation.14 | async-start | bytes 2097152 | tf_op jit(solution)/shard_map/all_to_all | solution.py:193
  385.6 12.4 %all-to-all-start.13 = ((bf16[8,8,128]{2,1,0:T(8,128)(2,1)}), bf16[8,8,128]{2,1,0:T(8,128)(2,1)S(1)}, u32[]{:S(2)}, u32[]{:S(2)}) async-start(bf16[8,8,128]{2,1,0:T(8,128)(2,1)} %bitcast.92), calls=%async_computation.13 | async-start | bytes 32768 | tf_op jit(solution)/shard_map/all_to_all | solution.py:225
  398.0 8.6 %all-to-all-start.15 = ((bf16[8,8,128]{2,1,0:T(8,128)(2,1)}), bf16[8,8,128]{2,1,0:T(8,128)(2,1)S(1)}, u32[]{:S(2)}, u32[]{:S(2)}) async-start(bf16[8,8,128]{2,1,0:T(8,128)(2,1)} %bitcast.95), calls=%async_computation.15 | async-start | bytes 32768 | tf_op jit(solution)/shard_map/all_to_all | solution.py:226
  (14 other events, 12.4 us)
where the time goes:
time: 410 us; the launch traced here: 408 us
  waiting for transfers between devices  103 us (25%)
  starting transfers between devices  93.5 us (23%)
  blocking collectives  90.9 us (22%)
  local copies, waits for them, and re-layouts  61.5 us (15%)
  matrix products  41.9 us (10%)
  other arithmetic  15.4 us (4%)
    all_to_all x1, blocking collectives, shards(): lax.all_to_all(slot_key_grads, 'ctx', split_axis=0, concat_axis=0, tiled=...  65.3 us
    all_to_all x1, waiting for transfers between devices, shards(): lax.all_to_all(slot_value_grads, 'ctx', split_axis=0, concat_axis=0, tile...  48.1 us
    all_to_all x1, blocking collectives, shards(): lax.all_to_all(clean_token_keys, 'head', split_axis=1, concat_axis=0, til...  14.9 us
    all_to_all x1, starting transfers between devices, shards(): lax.all_to_all(send_keys, 'ctx', split_axis=0, concat_axis=0, tiled=True)  14.2 us
    dot_general x5, matrix products, output_tile(): jnp.einsum('gqrk,kgd->qgrd', softmax_weights, tile_values, preferred_elem...  13.8 us
    ppermute x4, waiting for transfers between devices, swapped(): return lax.ppermute(block, axis, route)  12.7 us
    all_to_all x1, starting transfers between devices, shards(): lax.all_to_all(send_values, 'ctx', split_axis=0, concat_axis=0, tiled=True)  12.1 us
    all_to_all x1, blocking collectives, shards(): lax.all_to_all(attended.reshape(query_matrix_rows, key_value_groups * hea...  10.7 us
  transfers between devices with their start and end apart: 17, of which 13 were waited for; matrix products, arithmetic and copies ran while one was open for 27% of the time, Pallas kernels for 0%

commit v1 on v0

v1 whole, which is shorter than its diff:
```python
import functools

import jax
import jax.numpy as jnp
from jax import lax
from jax.experimental import pallas as pl
from jax.experimental.pallas import tpu as pltpu
from jax.sharding import PartitionSpec as P

BLK = 32
HEAD_SIZE = 128
SCALE = HEAD_SIZE**-0.5
LOG2E = 1.4426950408889634
NX = 4
F32 = jnp.float32
BF16 = jnp.bfloat16
MESH = pl.DeviceIdType.MESH
ANY = pl.BlockSpec(memory_space=pl.ANY)
VMEM = pl.BlockSpec(memory_space=pltpu.VMEM)
SMEM = pl.BlockSpec(memory_space=pltpu.SMEM)


class Place:
    def __init__(self, nz, nh):
        self.nz, self.nh = nz, nh
        ctx = lax.axis_index("ctx")
        self.head = lax.axis_index("head")
        self.x = ctx // nz
        self.z = ctx % nz
        self.right = nz // 2
        self.left = nz - 1 - nz // 2

    def wrap_x(self, d):
        return lax.rem(self.x + (d + NX), NX)

    def wrap_z(self, d):
        return lax.rem(self.z + (d + self.nz), self.nz)

    def wrap_head(self, d):
        return lax.rem(self.head + (d + self.nh), self.nh)

    def at(self, x, z, head):
        return (x * self.nz + z, head)

    def x_peer(self, d):
        return self.at(self.wrap_x(d), self.z, self.head)

    def z_peer(self, d):
        return self.at(self.x, self.wrap_z(d), self.head)

    def head_peer(self, d):
        return self.at(self.x, self.z, self.wrap_head(d))

    def partner_z(self):
        return self.z + 1 - 2 * lax.rem(self.z, 2)

    def partner(self, head):
        return self.at(self.x, self.partner_z(), head)


def greet(peers):
    barrier = pltpu.get_barrier_semaphore()
    for peer in peers:
        pl.semaphore_signal(barrier, inc=1, device_id=peer, device_id_type=MESH)
    pl.semaphore_wait(barrier, len(peers))


def remote(src, dst, send, recv, peer):
    return pltpu.make_async_remote_copy(
        src_ref=src, dst_ref=dst, send_sem=send, recv_sem=recv, device_id=peer, device_id_type=MESH
    )


def lanes(index, width):
    return pl.ds(pl.multiple_of(index * width, 128), width)


def gather_kernel(
    nz, nh, q, do, k, v, ck, cv, qg, dog, kn, vn, kv_out,
    kv, own_q, own_do, own_k, own_v,
    in_send, in_recv, own_sem, opp_sem, z_send, z_recv, x_send, x_recv, out_sem,
):
    me = Place(nz, nh)
    qw = q.shape[1] // nh
    kw = k.shape[1] // nh
    mine = me.head
    greet(
        [me.head_peer(d) for d in range(1, nh)]
        + [me.partner(me.wrap_head(d)) for d in range(nh)]
        + [me.z_peer(1), me.z_peer(-1), me.x_peer(1), me.x_peer(-1), me.x_peer(2)]
    )
    sends = []

    def go(copy):
        copy.start()
        sends.append(copy)
        return copy

    local = [
        pltpu.make_async_copy(ck.at[:, lanes(mine, kw)], kv.at[me.x, me.z, 0, mine], own_sem.at[0]),
        pltpu.make_async_copy(cv.at[:, lanes(mine, kw)], kv.at[me.x, me.z, 1, mine], own_sem.at[1]),
        pltpu.make_async_copy(k.at[:, lanes(mine, kw)], own_k, own_sem.at[2]),
        pltpu.make_async_copy(v.at[:, lanes(mine, kw)], own_v, own_sem.at[3]),
        pltpu.make_async_copy(q.at[:, lanes(mine, qw)], own_q, own_sem.at[4]),
        pltpu.make_async_copy(do.at[:, lanes(mine, qw)], own_do, own_sem.at[5]),
    ]
    for copy in local:
        copy.start()
    clean = []
    for d in range(1, nh):
        peer, to = me.head_peer(d), me.wrap_head(d)
        for i, src in enumerate((ck, cv)):
            clean.append(
                go(
                    remote(
                        src.at[:, lanes(to, kw)], kv.at[me.x, me.z, i, mine],
                        in_send.at[i, d], in_recv.at[i, d], peer,
                    )
                )
            )
    heads = []
    for d in range(nh):
        to = me.wrap_head(d)
        for i, (src, dst) in enumerate(((k, kn), (v, vn))):
            if d:
                heads.append(
                    go(
                        remote(
                            src.at[:, lanes(to, kw)], dst.at[0, mine],
                            in_send.at[2 + i, d], in_recv.at[2 + i, d], me.head_peer(d),
                        )
                    )
                )
            heads.append(
                go(
                    remote(
                        src.at[:, lanes(to, kw)], dst.at[1, mine],
                        in_send.at[4 + i, d], in_recv.at[4 + i, d], me.partner(to),
                    )
                )
            )
    for i, (src, dst) in enumerate(((q, qg), (do, dog))):
        for d in range(1, nh):
            to = me.wrap_head(d)
            heads.append(
                go(
                    remote(
                        src.at[:, lanes(to, qw)], dst.at[mine],
                        in_send.at[6 + i, d], in_recv.at[6 + i, d], me.head_peer(d),
                    )
                )
            )
    for copy in local[:2]:
        copy.wait()
    for copy in clean:
        copy.wait_recv()

    opposite = me.wrap_x(2)
    mine_unit = kv.at[me.x, me.z]
    first_opp = go(remote(mine_unit, mine_unit, opp_sem.at[0], opp_sem.at[1], me.x_peer(2)))
    columns = (me.x, opposite)
    sideways = []

    def pass_on(z, slot):
        for i, d in enumerate((1, -1)):
            sideways.append(
                go(remote(kv.at[me.x, z], kv.at[me.x, z], x_send.at[i, slot], x_recv.at[i, slot], me.x_peer(d)))
            )

    def hop(direction, unit, step):
        z = me.wrap_z(-step if direction == 0 else step)
        ref = kv.at[columns[unit], z]
        return go(
            remote(
                ref, ref, z_send.at[direction, unit, step], z_recv.at[direction, unit, step],
                me.z_peer(1 if direction == 0 else -1),
            )
        )

    steps = (me.right, me.left)
    flying = {}
    for step in range(max(steps) + 1):
        for unit in (0, 1):
            if step == 0 and unit == 1:
                first_opp.wait_recv()
            for direction in (0, 1):
                if step > 0 and step - 1 < steps[direction]:
                    flying[direction, unit].wait_recv()
                if step < steps[direction]:
                    flying[direction, unit] = hop(direction, unit, step)
            if unit == 0:
                if step == 0:
                    pass_on(me.z, 0)
                else:
                    for direction in (0, 1):
                        if step - 1 < steps[direction]:
                            z = me.wrap_z(-step if direction == 0 else step)
                            pass_on(z, step if direction == 0 else me.right + step)
        if step == 1:
            for copy in local[2:]:
                copy.wait()
            back = [
                pltpu.make_async_copy(own_k, kn.at[0, mine], own_sem.at[0]),
                pltpu.make_async_copy(own_v, vn.at[0, mine], own_sem.at[1]),
                pltpu.make_async_copy(own_q, qg.at[mine], own_sem.at[2]),
                pltpu.make_async_copy(own_do, dog.at[mine], own_sem.at[3]),
            ]
            for copy in back:
                copy.start()
    outs = [
        pltpu.make_async_copy(kv.at[x], kv_out.at[x], out_sem.at[i]) for i, x in enumerate(columns)
    ]
    for copy in outs:
        copy.start()
    for copy in sideways:
        copy.wait_recv()
    for i, d in enumerate((1, -1)):
        x = me.wrap_x(d)
        outs.append(pltpu.make_async_copy(kv.at[x], kv_out.at[x], out_sem.at[2 + i]))
        outs[-1].start()
    for copy in heads:
        copy.wait_recv()
    for copy in sends:
        copy.wait_send()
    for copy in back + outs:
        copy.wait()


def gather(nz, nh, q, do, k, v, ck, cv):
    rows, qw, kw, crows = q.shape[0], q.shape[1] // nh, k.shape[1] // nh, ck.shape[0]
    dma = pltpu.SemaphoreType.DMA
    return pl.pallas_call(
        functools.partial(gather_kernel, nz, nh),
        out_shape=(
            jax.ShapeDtypeStruct((nh, rows, qw), BF16),
            jax.ShapeDtypeStruct((nh, rows, qw), BF16),
            jax.ShapeDtypeStruct((2, nh, rows, kw), BF16),
            jax.ShapeDtypeStruct((2, nh, rows, kw), BF16),
            jax.ShapeDtypeStruct((NX, nz, 2, nh, crows, kw), BF16),
        ),
        in_specs=[ANY] * 6,
        out_specs=(ANY,) * 5,
        scratch_shapes=[
            pltpu.VMEM((NX, nz, 2, nh, crows, kw), BF16),
            pltpu.VMEM((rows, qw), BF16),
            pltpu.VMEM((rows, qw), BF16),
            pltpu.VMEM((rows, kw), BF16),
            pltpu.VMEM((rows, kw), BF16),
            dma((8, nh)),
            dma((8, nh)),
            dma((6,)),
            dma((2,)),
            dma((2, 2, nz // 2)),
            dma((2, 2, nz // 2)),
            dma((2, nz)),
            dma((2, nz)),
            dma((4,)),
        ],
        compiler_params=pltpu.CompilerParams(collective_id=0, has_side_effects=True),
        name="gather",
    )(q, do, k, v, ck, cv)


def dot(a, b, dim_a, dim_b):
    return lax.dot_general(a, b, (((dim_a,), (dim_b,)), ((), ())), preferred_element_type=F32)


def attention_kernel(
    listed, live, q_ref, do_ref, kn_ref, vn_ref, kv_ref,
    o_ref, dq_ref, dk_own, dv_own, dk_other, dv_other, dkv_ref,
    keys, values, bias, qs, dos, weights, dscores, acc,
):
    span = kn_ref.shape[0]
    rows = span // 2
    stores = kv_ref.shape[0]
    heads = q_ref.shape[1] // HEAD_SIZE
    keys[0:span] = kn_ref[...]
    values[0:span] = vn_ref[...]

    def fetch(s, carry):
        b = jnp.maximum(listed[s], 0)
        at = pl.ds(pl.multiple_of(span + s * BLK, BLK), BLK)
        keys[at] = kv_ref[s, 0, b]
        values[at] = kv_ref[s, 1, b]
        return carry

    lax.fori_loop(0, stores, fetch, 0, unroll=4)
    width = stores * BLK
    spread = lax.broadcasted_iota(jnp.int32, (stores, width), 1) // BLK == lax.broadcasted_iota(
        jnp.int32, (stores, width), 0
    )
    dead = (live[...] < 0).astype(F32)
    bias[:, 0:span] = jnp.zeros((1, span), F32)
    bias[:, span:] = dot(dead, spread.astype(F32), 1, 0) * -1e30

    def head(r, carry):
        col = lanes(r, HEAD_SIZE)
        q, do = q_ref[:, col], do_ref[:, col]
        t = dot(q, keys[...], 1, 1) * (SCALE * LOG2E) + bias[...]
        e = jnp.exp2(t - jnp.max(t, -1, keepdims=True))
        p = e * (1.0 / jnp.sum(e, -1, keepdims=True))
        w = p.astype(BF16)
        o = dot(w, values[...], 1, 0).astype(BF16)
        o_ref[:, col] = o
        row_dot = jnp.sum(do.astype(F32) * o.astype(F32), -1, keepdims=True)
        ds = (p * (dot(do, values[...], 1, 1) - row_dot)).astype(BF16)
        dq_ref[:, col] = (dot(ds, keys[...], 1, 0) * SCALE).astype(BF16)
        at = pl.ds(pl.multiple_of(r * rows, rows), rows)
        qs[at], dos[at], weights[at], dscores[at] = q, do, w, ds
        return carry

    lax.fori_loop(0, heads, head, 0)

    def emit(left, right, scale, own, other, i):
        g = dot(right[...], left[...], 0, 0).T
        if scale is not None:
            g = g * scale
        own[...] = g[0:rows]
        other[...] = g[rows:span].astype(BF16)
        acc[...] = g[span:].reshape(stores, BLK, HEAD_SIZE)

        def put(s, carry):
            value, b = acc[s], listed[s]
            for block in (0, 1):
                dkv_ref[s, i, block] = jnp.where(b == block, value, 0.0).astype(BF16)
            return carry

        lax.fori_loop(0, stores, put, 0, unroll=4)

    emit(dscores, qs, SCALE, dk_own, dk_other, 0)
    emit(weights, dos, None, dv_own, dv_other, 1)


def attention(listed, live, q, do, kn, vn, kv):
    rows, span, stores = q.shape[0], kn.shape[0], kv.shape[0]
    count = span + stores * BLK
    stacked = rows * (q.shape[1] // HEAD_SIZE)
    half = (span // 2, HEAD_SIZE)
    return pl.pallas_call(
        attention_kernel,
        out_shape=(
            jax.ShapeDtypeStruct(q.shape, BF16),
            jax.ShapeDtypeStruct(q.shape, BF16),
            jax.ShapeDtypeStruct(half, F32),
            jax.ShapeDtypeStruct(half, F32),
            jax.ShapeDtypeStruct(half, BF16),
            jax.ShapeDtypeStruct(half, BF16),
            jax.ShapeDtypeStruct(kv.shape, BF16),
        ),
        in_specs=[SMEM] + [VMEM] * 6,
        out_specs=(VMEM,) * 7,
        scratch_shapes=[
            pltpu.VMEM((count, HEAD_SIZE), BF16),
            pltpu.VMEM((count, HEAD_SIZE), BF16),
            pltpu.VMEM((1, count), F32),
            pltpu.VMEM((stacked, HEAD_SIZE), BF16),
            pltpu.VMEM((stacked, HEAD_SIZE), BF16),
            pltpu.VMEM((stacked, count), BF16),
            pltpu.VMEM((stacked, count), BF16),
            pltpu.VMEM((stores, BLK, HEAD_SIZE), F32),
        ],
        compiler_params=pltpu.CompilerParams(vmem_limit_bytes=60 * 2**20),
        name="attention",
    )(listed, live, q, do, kn, vn, kv)


def return_kernel(
    nz, nh, o, dq, dk_own, dv_own, dk_other, dv_other, dkv,
    o_out, dq_out, dk_out, dv_out, dck_out, dcv_out,
    from_x, ring_in, ring_out, opp_out, opp_in, pair_in, noisy, final, own_o, own_dq,
    out_send, out_recv, own_sem, pair_send, pair_recv, x_send, x_recv, z_send, z_recv, opp_sem,
):
    me = Place(nz, nh)
    mine = me.head
    qw, kw = o.shape[2], noisy.shape[3]
    greet(
        [me.head_peer(d) for d in range(1, nh)]
        + [me.partner(mine), me.z_peer(1), me.z_peer(-1), me.x_peer(1), me.x_peer(-1), me.x_peer(2)]
    )
    sends, heads = [], []

    def go(copy):
        copy.start()
        sends.append(copy)
        return copy

    order = [me.right]
    for far in range(me.right - 1, 0, -1):
        order += [far, -far]
    if me.left == me.right:
        order.insert(1, -me.right)
    order.append(0)
    sideways = {}
    for slot, far in enumerate(order):
        z = me.wrap_z(far)
        for i, d in enumerate((1, -1)):
            x = me.wrap_x(d)
            sideways[far, i] = go(
                remote(dkv.at[x, z], from_x.at[i, slot], x_send.at[i, slot], x_recv.at[i, slot], me.x_peer(d))
            )
    pair = [
        go(remote(src, pair_in.at[i], pair_send.at[i], pair_recv.at[i], me.partner(mine)))
        for i, src in enumerate((dk_other, dv_other))
    ]
    local = [
        pltpu.make_async_copy(o.at[mine], own_o, own_sem.at[0]),
        pltpu.make_async_copy(dq.at[mine], own_dq, own_sem.at[1]),
    ]
    for copy in local:
        copy.start()
    for i, (src, dst) in enumerate(((o, o_out), (dq, dq_out))):
        for d in range(1, nh):
            heads.append(
                go(
                    remote(
                        src.at[me.wrap_head(d)], dst.at[:, lanes(mine, qw)],
                        out_send.at[i, d], out_recv.at[i, d], me.head_peer(d),
                    )
                )
            )

    opposite = me.wrap_x(2)

    def term(unit, far):
        z = me.wrap_z(far)
        if unit == 1:
            return dkv[opposite, z].astype(F32)
        slot = order.index(far)
        for i in (0, 1):
            sideways[far, i].wait_recv()
        return dkv[me.x, z].astype(F32) + from_x[0, slot].astype(F32) + from_x[1, slot].astype(F32)

    steps = (me.right, me.left)
    flying = {}

    def noisy_sums():
        for i, own in enumerate((dk_own, dv_own)):
            pair[i].wait_recv()
            noisy[i] = (own[...] + pair_in[i].astype(F32)).astype(BF16)

    def noisy_out():
        for i, dst in enumerate((dk_out, dv_out)):
            for d in range(1, nh):
                heads.append(
                    go(
                        remote(
                            noisy.at[i, me.wrap_head(d)], dst.at[:, lanes(mine, kw)],
                            out_send.at[2 + i, d], out_recv.at[2 + i, d], me.head_peer(d),
                        )
                    )
                )

    for step in range(me.right):
        for unit in (1, 0):
            for direction in (0, 1):
                if step >= steps[direction]:
                    continue
                far = (steps[direction] - step) * (1 if direction == 0 else -1)
                total = term(unit, far)
                if step:
                    flying[direction, unit].wait_recv()
                    total = total + ring_in[direction, unit, step - 1].astype(F32)
                ring_out[direction, unit, step] = total.astype(BF16)
            for direction in (0, 1):
                if step >= steps[direction]:
                    continue
                flying[direction, unit] = go(
                    remote(
                        ring_out.at[direction, unit, step], ring_in.at[direction, unit, step],
                        z_send.at[direction, unit, step], z_recv.at[direction, unit, step],
                        me.z_peer(1 if direction == 0 else -1),
                    )
                )
        if step == 0:
            for copy in local:
                copy.wait()
            local = [
                pltpu.make_async_copy(own_o, o_out.at[:, lanes(mine, qw)], own_sem.at[0]),
                pltpu.make_async_copy(own_dq, dq_out.at[:, lanes(mine, qw)], own_sem.at[1]),
            ]
            for copy in local:
                copy.start()
            noisy_sums()
        if step == min(1, me.right - 1):
            noisy_out()
            for i, dst in enumerate((dk_out, dv_out)):
                local.append(
                    pltpu.make_async_copy(noisy.at[i, mine], dst.at[:, lanes(mine, kw)], own_sem.at[2 + i])
                )
                local[-1].start()

    def arrived(unit):
        total = term(unit, 0)
        for direction in (0, 1):
            if steps[direction]:
                flying[direction, unit].wait_recv()
                total = total + ring_in[direction, unit, steps[direction] - 1].astype(F32)
        return total

    opp_out[...] = arrived(1).astype(BF16)
    own_total = arrived(0)
    across = go(remote(opp_out, opp_in, opp_sem.at[0], opp_sem.at[1], me.x_peer(2)))
    across.wait_recv()
    final[...] = (own_total + opp_in[...].astype(F32)).astype(BF16)
    for d in range(1, nh):
        for i, dst in enumerate((dck_out, dcv_out)):
            heads.append(
                go(
                    remote(
                        final.at[i, me.wrap_head(d)], dst.at[:, lanes(mine, kw)],
                        out_send.at[4 + i, d], out_recv.at[4 + i, d], me.head_peer(d),
                    )
                )
            )
    for i, dst in enumerate((dck_out, dcv_out)):
        local.append(pltpu.make_async_copy(final.at[i, mine], dst.at[:, lanes(mine, kw)], own_sem.at[4 + i]))
        local[-1].start()
    for copy in heads:
        copy.wait_recv()
    for copy in sends:
        copy.wait_send()
    for copy in local:
        copy.wait()


def give_back(nz, nh, o, dq, dk_own, dv_own, dk_other, dv_other, dkv):
    rows, qw, kw, crows = o.shape[1], o.shape[2], dk_own.shape[2], dkv.shape[4]
    dma = pltpu.SemaphoreType.DMA
    wide = jax.ShapeDtypeStruct((rows, nh * qw), BF16)
    narrow = jax.ShapeDtypeStruct((rows, nh * kw), BF16)
    clean = jax.ShapeDtypeStruct((crows, nh * kw), BF16)
    half = nz // 2
    unit = (2, nh, crows, kw)
    return pl.pallas_call(
        functools.partial(return_kernel, nz, nh),
        out_shape=(wide, wide, narrow, narrow, clean, clean),
        in_specs=[ANY, ANY] + [VMEM] * 5,
        out_specs=(ANY,) * 6,
        scratch_shapes=[
            pltpu.VMEM((2, nz) + unit, BF16),
            pltpu.VMEM((2, 2, half) + unit, BF16),
            pltpu.VMEM((2, 2, half) + unit, BF16),
            pltpu.VMEM(unit, BF16),
            pltpu.VMEM(unit, BF16),
            pltpu.VMEM((2, nh, rows, kw), BF16),
            pltpu.VMEM((2, nh, rows, kw), BF16),
            pltpu.VMEM(unit, BF16),
            pltpu.VMEM((rows, qw), BF16),
            pltpu.VMEM((rows, qw), BF16),
            dma((6, nh)),
            dma((6, nh)),
            dma((6,)),
            dma((2,)),
            dma((2,)),
            dma((2, nz)),
            dma((2, nz)),
            dma((2, 2, half)),
            dma((2, 2, half)),
            dma((2,)),
        ],
        compiler_params=pltpu.CompilerParams(collective_id=1, has_side_effects=True),
        name="give_back",
    )(o, dq, dk_own, dv_own, dk_other, dv_other, dkv)


def shards(nz, nh, queries, nk, nv, ck, cv, output_gradient, history_list):
    qg, dog, kn, vn, kv = gather(nz, nh, queries, output_gradient, nk, nv, ck, cv)
    rows = nh * queries.shape[0]
    stores = NX * nz
    listed = lax.dynamic_index_in_dim(history_list, lax.axis_index("ctx"), 0, keepdims=False)
    o, dq, dk_own, dv_own, dk_other, dv_other, dkv = attention(
        listed,
        listed[None],
        qg.reshape(rows, -1),
        dog.reshape(rows, -1),
        kn.reshape(2 * rows, HEAD_SIZE),
        vn.reshape(2 * rows, HEAD_SIZE),
        kv.reshape(stores, 2, -1, BLK, HEAD_SIZE),
    )
    noisy = (nh, queries.shape[0], HEAD_SIZE)
    return give_back(
        nz,
        nh,
        o.reshape(qg.shape),
        dq.reshape(qg.shape),
        dk_own.reshape(noisy),
        dv_own.reshape(noisy),
        dk_other.reshape(noisy),
        dv_other.reshape(noisy),
        dkv.reshape(kv.shape),
    )


def solution(mesh):
    nz, nh = mesh.shape["ctx"] // NX, mesh.shape["head"]
    tokens = P(("ctx", "head"), None)
    return jax.shard_map(
        functools.partial(shards, nz, nh),
        mesh=mesh,
        in_specs=(tokens,) * 6 + (P(),),
        out_specs=(tokens,) * 6,
        check_vma=False,
    )
```

time: 410 us -> 130 us (0.32)
  Pallas kernels: 0 us -> 118 us
  waiting for transfers between devices: 103 us -> 0 us
  starting transfers between devices: 93.5 us -> 0 us
  blocking collectives: 90.9 us -> 0 us
  local copies, waits for them, and re-layouts: 61.5 us -> 10.7 us
  matrix products: 41.9 us -> 0 us
  other arithmetic: 15.4 us -> 0 us
    pallas_call x0 -> x3, Pallas kernels: none -> 118 us  [the longest x1 52.7 us: give_back(): pl.pallas_call(functools.partial(return_kernel, nz, nh), out_shape=(wide,...]
    all_to_all x3 -> x0, blocking collectives: 90.9 us -> none  [the longest x1 65.3 us: shards(): lax.all_to_all(slot_key_grads, 'ctx', split_axis=0, concat_axis=0, tiled=...]
    all_to_all x13 -> x0, waiting for transfers between devices: 90.3 us -> none  [the longest x1 48.1 us: shards(): lax.all_to_all(slot_value_grads, 'ctx', split_axis=0, concat_axis=0, tile...]
    all_to_all x13 -> x0, starting transfers between devices: 82.8 us -> none  [the longest x1 14.2 us: shards(): lax.all_to_all(send_keys, 'ctx', split_axis=0, concat_axis=0, tiled=True)]
    dot_general x36 -> x0, matrix products: 41.9 us -> none  [the longest x5 13.8 us: output_tile(): jnp.einsum('gqrk,kgd->qgrd', softmax_weights, tile_values, preferred_elem...]
    ppermute x4 -> x0, waiting for transfers between devices: 12.7 us -> none  [swapped(): return lax.ppermute(block, axis, route)]
    dynamic_slice x28 -> x1, local copies, waits for them, and re-layouts: 12.4 us -> 0.51 us  [shards(): lax.dynamic_index_in_dim(history_list, lax.axis_index('ctx'), 0, keepdims...]
    reshape x14 -> x0, local copies, waits for them, and re-layouts: 11 us -> none  [the longest x12 10.3 us: clean_tile(): jnp.repeat(lax.dynamic_slice_in_dim(live_slots, first_slot, slot_group, 0...]
  transfers between devices with their start and end apart: 17 -> 0, of which waited for: 13 -> 0; matrix products, arithmetic and copies ran while one was open for 27% -> 0% of each run, Pallas kernels for 0% -> 0%
where the time goes in v1:
time: 130 us; the launch traced here: 129 us
  Pallas kernels  118 us (91%)
  local copies, waits for them, and re-layouts  10.7 us (8%)
    pallas_call x1, Pallas kernels, give_back(): pl.pallas_call(functools.partial(return_kernel, nz, nh), out_shape=(wide,...  52.7 us
    pallas_call x1, Pallas kernels, gather(): pl.pallas_call(functools.partial(gather_kernel, nz, nh), out_shape=(jax.S...  47.3 us
    pallas_call x1, Pallas kernels, attention(): pl.pallas_call(attention_kernel, out_shape=(jax.ShapeDtypeStruct(q.shape,...  17.6 us
    unnamed x8, local copies, waits for them, and re-layouts  9.63 us

profile of v1, /device:TPU:1, one launch (start us, length us, event | category | flops | bytes accessed | tf_op | source)
XLA Modules:
  0.0 128.9 jit_solution(6299734398271833700)
XLA Ops:
  0.6 0.0 copy-start
  0.7 0.7 copy-done
  1.4 0.5 fusion.listed
  1.9 0.5 constant_dynamic-slice_fusion.live
  2.4 47.3 %gather.1 = (bf16[8,24,768]{2,1,0:T(8,128)(2,1)}, bf16[8,24,768]{2,1,0:T(8,128)(2,1)}, bf16[2,8,24,128]{3,2,1,0:T(8,128)(2,1)}, bf16[2,8,24,128]{3,2,1,0:T(8,128)(2,1)}, bf16[4,16,2,8,8,128]{5,4,3,2,1,0:T(8,128)(2,1)}) custom-call(bf16[24,6144]{1,0:T(8,128)(2,1)} %q.1, bf16[24,6144]{1,0:T(8,128)(2,1)} %do.1, bf16[24,1024]{1,0:T(8,128)(2,1)} %k.1, ...), custom_call_target="tpu_custom_call" | custom-call | tf_op jit(solution)/shard_map/gather/pallas_call | solution.py:232
  49.7 17.6 %attention.1 = (bf16[192,768]{1,0:T(8,128)(2,1)}, bf16[192,768]{1,0:T(8,128)(2,1)}, f32[192,128]{1,0:T(8,128)}, f32[192,128]{1,0:T(8,128)}, bf16[192,128]{1,0:T(...) custom-call(s32[64]{0:T(128)} %fusion.listed, s32[1,64]{1,0:T(1,128)} %constant_dynamic-slice_fusion.live, ...), custom_call_target="tpu_custom_call" | custom-call | tf_op jit(solution)/shard_map/attention/pallas_call | solution.py:339
  67.4 52.7 %give_back.1 = (bf16[24,6144]{1,0:T(8,128)(2,1)}, bf16[24,6144]{1,0:T(8,128)(2,1)}, bf16[24,1024]{1,0:T(8,128)(2,1)}, bf16[24,1024]{1,0:T(8,128)(2,1)}, bf16[8,1...) custom-call(bf16[8,24,768]{2,1,0:T(8,128)(2,1)} %bitcast.16, bf16[8,24,768]{2,1,0:T(8,128)(2,1)} %bitcast.17, ...), custom_call_target="tpu_custom_call" | custom-call | tf_op jit(solution)/shard_map/give_back/pallas_call | solution.py:534
  120.1 1.7 %copy.19 = bf16[24,6144]{1,0:T(8,128)(2,1)} copy(bf16[24,6144]{1,0:T(8,128)(2,1)} %get-tuple-element.36) | data formatting | bytes 589824
  121.8 1.7 %copy.20 = bf16[24,6144]{1,0:T(8,128)(2,1)} copy(bf16[24,6144]{1,0:T(8,128)(2,1)} %get-tuple-element.37) | data formatting | bytes 589824
  123.5 1.4 %copy.21 = bf16[24,1024]{1,0:T(8,128)(2,1)} copy(bf16[24,1024]{1,0:T(8,128)(2,1)} %get-tuple-element.38) | data formatting | bytes 98304
  124.9 1.4 %copy.22 = bf16[24,1024]{1,0:T(8,128)(2,1)} copy(bf16[24,1024]{1,0:T(8,128)(2,1)} %get-tuple-element.39) | data formatting | bytes 98304
  126.3 1.3 %copy.23 = bf16[8,1024]{1,0:T(8,128)(2,1)} copy(bf16[8,1024]{1,0:T(8,128)(2,1)} %get-tuple-element.40) | data formatting | bytes 32768
  127.6 1.3 %copy.24 = bf16[8,1024]{1,0:T(8,128)(2,1)} copy(bf16[8,1024]{1,0:T(8,128)(2,1)} %get-tuple-element.41) | data formatting | bytes 32768
Async XLA Ops:
  0.6 0.8 copy-start

commit v2 on v0

v2 whole, which is shorter than its diff:
```python
import functools

import jax
import jax.numpy as jnp
from jax import lax
from jax.experimental import pallas as pl
from jax.experimental.pallas import tpu as pltpu
from jax.sharding import PartitionSpec as P

BLK = 32
HEAD_SIZE = 128
SCALE = HEAD_SIZE**-0.5
LOG2E = 1.4426950408889634
NX = 4
F32 = jnp.float32
BF16 = jnp.bfloat16
MESH = pl.DeviceIdType.MESH
ANY = pl.BlockSpec(memory_space=pl.ANY)
VMEM = pl.BlockSpec(memory_space=pltpu.VMEM)
SMEM = pl.BlockSpec(memory_space=pltpu.SMEM)


class Place:
    def __init__(self, nz, nh):
        self.nz, self.nh = nz, nh
        ctx = lax.axis_index("ctx")
        self.head = lax.axis_index("head")
        self.x = ctx // nz
        self.z = ctx % nz
        self.right = nz // 2
        self.left = nz - 1 - nz // 2

    def wrap_x(self, d):
        return lax.rem(self.x + (d + NX), NX)

    def wrap_z(self, d):
        return lax.rem(self.z + (d + self.nz), self.nz)

    def wrap_head(self, d):
        return lax.rem(self.head + (d + self.nh), self.nh)

    def at(self, x, z, head):
        return (x * self.nz + z, head)

    def x_peer(self, d):
        return self.at(self.wrap_x(d), self.z, self.head)

    def z_peer(self, d):
        return self.at(self.x, self.wrap_z(d), self.head)

    def head_peer(self, d):
        return self.at(self.x, self.z, self.wrap_head(d))

    def z_peers(self):
        return [self.z_peer(d) for d in (1, -1) + ((2, -2) if self.right > 1 else ())]

    def partner_z(self):
        return self.z + 1 - 2 * lax.rem(self.z, 2)

    def partner(self, head):
        return self.at(self.x, self.partner_z(), head)


def greet(peers):
    barrier = pltpu.get_barrier_semaphore()
    for peer in peers:
        pl.semaphore_signal(barrier, inc=1, device_id=peer, device_id_type=MESH)
    pl.semaphore_wait(barrier, len(peers))


def remote(src, dst, send, recv, peer):
    return pltpu.make_async_remote_copy(
        src_ref=src, dst_ref=dst, send_sem=send, recv_sem=recv, device_id=peer, device_id_type=MESH
    )


def lanes(index, width):
    return pl.ds(pl.multiple_of(index * width, 128), width)


def dot(a, b, dim_a, dim_b):
    return lax.dot_general(a, b, (((dim_a,), (dim_b,)), ((), ())), preferred_element_type=F32)


SIDES = (0, 1, -1, 2)
OWN, RIGHT, LEFT, FAR = range(4)


def kernel(
    nz, nh, listed, q, do, k, v, ck, cv,
    o_out, dq_out, dk_out, dv_out, dck_out, dcv_out, qg, dog, kn, vn, og, dqg, ng,
    kv, own_q, own_do, own_k, own_v, q_all, do_all, o_all, dq_all, qs, dos, keys, values,
    t, dp, peak, weights, dscores, bias, terms, relay_in, relay_out, from_x, ring_in, ring_out,
    other, pair_in, span_grad, noisy_sum, final,
    in_send, in_recv, own_sem, load_sem, gz_send, gz_recv, gx_send, gx_recv,
    out_send, out_recv, put_sem, pair_send, pair_recv, x_send, x_recv, z_send, z_recv,
):
    me = Place(nz, nh)
    mine = me.head
    qw, kw = q.shape[1] // nh, k.shape[1] // nh
    few = q.shape[0]
    rows = few * nh
    span = 2 * rows
    heads = qw // HEAD_SIZE
    half = nz // 2
    width = half * BLK
    reach = (me.right, me.left)
    offsets = [0] + [d * sign for d in range(1, half) for sign in (1, -1)] + [half]
    slot_of = {off: p for p, off in enumerate(offsets)}
    slot_of[-half] = slot_of[half]

    sends = []

    def go(copy):
        copy.start()
        sends.append(copy)
        return copy

    def token_rows(index):
        return pl.ds(pl.multiple_of(index * few, 8), few)

    local = [
        pltpu.make_async_copy(ck.at[:, lanes(mine, kw)], kv.at[OWN, 0, 0, mine], own_sem.at[0]),
        pltpu.make_async_copy(cv.at[:, lanes(mine, kw)], kv.at[OWN, 0, 1, mine], own_sem.at[1]),
        pltpu.make_async_copy(k.at[:, lanes(mine, kw)], own_k, own_sem.at[2]),
        pltpu.make_async_copy(v.at[:, lanes(mine, kw)], own_v, own_sem.at[3]),
        pltpu.make_async_copy(q.at[:, lanes(mine, qw)], own_q, own_sem.at[4]),
        pltpu.make_async_copy(do.at[:, lanes(mine, qw)], own_do, own_sem.at[5]),
    ]
    for copy in local:
        copy.start()
    greet([me.head_peer(d) for d in range(1, nh)] + me.z_peers() + [me.x_peer(1), me.x_peer(-1)])

    def spread(which, src, dst_at, size):
        copies = []
        for d in range(1, nh):
            copies.append(
                go(
                    remote(
                        src.at[:, lanes(me.wrap_head(d), size)], dst_at(mine),
                        in_send.at[which, d], in_recv.at[which, d], me.head_peer(d),
                    )
                )
            )
        return copies

    clean = [spread(i, src, lambda j, i=i: kv.at[OWN, 0, i, j], kw) for i, src in enumerate((ck, cv))]
    noisy = [spread(2 + i, src, lambda j, dst=dst: dst.at[token_rows(j)], kw) for i, (src, dst) in enumerate(((k, kn), (v, vn)))]
    wide = [spread(4 + i, src, lambda j, dst=dst: dst.at[token_rows(j)], qw) for i, (src, dst) in enumerate(((q, qg), (do, dog)))]
    for copy in local[:2] :
        copy.wait()
    for copy in sum(clean, []):
        copy.wait_recv()

    arriving, sideways, across = {}, {}, {}

    def source(direction, far):
        return slot_of[-far if direction == 0 else far]

    def hop(direction, far, stride):
        arriving[direction, far + stride] = go(
            remote(
                kv.at[OWN, source(direction, far)], kv.at[OWN, source(direction, far + stride)],
                gz_send.at[direction, far + stride], gz_recv.at[direction, far + stride],
                me.z_peer(stride if direction == 0 else -stride),
            )
        )

    def pass_on(p):
        for i, (d, side) in enumerate(((1, LEFT), (-1, RIGHT))):
            sideways[p, i] = go(
                remote(kv.at[OWN, p], kv.at[side, p], gx_send.at[i, p], gx_recv.at[i, p], me.x_peer(d))
            )

    def hand_over(p):
        for i in (0, 1):
            sideways[p, i].wait_recv()
        side, d = (RIGHT, -1) if p % 2 else (LEFT, 1)
        across[p] = go(remote(kv.at[side, p], kv.at[FAR, p], gx_send.at[2, p], gx_recv.at[2, p], me.x_peer(d)))

    def block_of(side, p):
        return listed[me.wrap_x(SIDES[side]) * nz + me.wrap_z(offsets[p])]

    def column(side, part):
        return span + side * nz * BLK + part * width

    def score(low, count):
        kk, vv = keys[low : low + count], values[low : low + count]

        def body(r, carry):
            at = pl.ds(pl.multiple_of(r * rows, rows), rows)
            s = dot(qs[at], kk, 1, 1) * (SCALE * LOG2E) + bias[:, low : low + count]
            t[at, low : low + count] = s
            dp[at, low : low + count] = dot(dos[at], vv, 1, 1)
            top = peak[at]
            if count % HEAD_SIZE:
                top = jnp.maximum(top, jnp.max(s, -1, keepdims=True))
            else:
                for j in range(0, count, HEAD_SIZE):
                    top = jnp.maximum(top, s[:, j : j + HEAD_SIZE])
            peak[at] = top
            return carry

        lax.fori_loop(0, heads, body, 0)

    def score_clean(side, part):
        low = column(side, part)
        place = lax.broadcasted_iota(jnp.int32, (1, width), 1) // BLK
        dead = jnp.zeros((1, width), F32)
        for j in range(half):
            p = part * half + j
            b = block_of(side, p)
            for i, dst in enumerate((keys, values)):
                both = kv[side, p, i].astype(F32).reshape(2 * BLK, kw)
                dst[low + j * BLK : low + (j + 1) * BLK] = jnp.where(b == 1, both[BLK:], both[:BLK]).astype(BF16)
            dead = jnp.where(place == j, jnp.where(b < 0, -1e30, 0.0), dead)
        bias[:, low : low + width] = dead
        score(low, width)

    def score_noisy():
        for copy in back + loads:
            copy.wait()
        for copy in pair_kv:
            copy.wait_recv()
        pulls = [pltpu.make_async_copy(src, dst.at[0:span], load_sem.at[2 + i]) for i, (src, dst) in enumerate(((kn, keys), (vn, values)))]
        for copy in pulls:
            copy.start()
        for r in range(heads):
            at, col = slice(r * rows, (r + 1) * rows), slice(r * HEAD_SIZE, (r + 1) * HEAD_SIZE)
            qs[at] = q_all[:, col]
            dos[at] = do_all[:, col]
        bias[:, 0:span] = jnp.zeros((1, span), F32)
        peak[...] = jnp.full(peak.shape, -3e38, F32)
        for copy in pulls:
            copy.wait()
        score(0, span)

    rounds = [[(0, 0)]]
    for near in range(1, me.right + 1, 2):
        rounds.append([(w, far) for far in (near, near + 1) for w in (0, 1) if far <= reach[w]])

    def advance(r):
        for direction, far in rounds[r]:
            if r == 0:
                for stride in (1, 2):
                    for w in (0, 1):
                        if stride <= reach[w]:
                            hop(w, 0, stride)
            else:
                arriving[direction, far].wait_recv()
                if far + 2 <= reach[direction]:
                    hop(direction, far, 2)
            pass_on(source(direction, far))

    def hand_round(r):
        for unit in rounds[r]:
            hand_over(source(*unit))

    last = len(rounds) - 1
    for r in range(last + 1):
        advance(r)
        if r == min(1, last):
            for copy in local[2:]:
                copy.wait()
            back = [
                pltpu.make_async_copy(src, dst.at[token_rows(mine)], own_sem.at[i])
                for i, (src, dst) in enumerate(((own_k, kn), (own_v, vn), (own_q, qg), (own_do, dog)))
            ]
            for copy in back:
                copy.start()
        if r == min(2, last):
            for copy in sum(noisy, []):
                copy.wait_recv()
            for copy in back:
                copy.wait()
            back = []
            pair_kv = [
                go(
                    remote(
                        ref.at[0:rows], ref.at[rows:span], in_send.at[6 + i, 0], in_recv.at[6 + i, 0],
                        me.partner(mine),
                    )
                )
                for i, ref in enumerate((kn, vn))
            ]
            for copy in sum(wide, []):
                copy.wait_recv()
            loads = [pltpu.make_async_copy(src, dst, load_sem.at[i]) for i, (src, dst) in enumerate(((qg, q_all), (dog, do_all)))]
            for copy in loads:
                copy.start()
        if r >= 2:
            hand_round(r - 2)
        if r == max(last - 1, min(2, last)):
            score_noisy()
            if last > 2:
                score_clean(OWN, 0)
    if last <= 2:
        score_clean(OWN, 0)
    if last > 0:
        hand_round(last - 1)
    score_clean(OWN, 1)
    done = sum(len(units) for units in rounds[:last])
    early = done >= half
    if early:
        score_clean(RIGHT, 0)
        score_clean(LEFT, 0)
    hand_round(last)
    if not early:
        score_clean(RIGHT, 0)
        score_clean(LEFT, 0)
    score_clean(RIGHT, 1)
    score_clean(LEFT, 1)
    for part in (0, 1):
        for p in range(part * half, (part + 1) * half):
            across[p].wait_recv()
        score_clean(FAR, part)

    def finish(r, carry):
        at = pl.ds(pl.multiple_of(r * rows, rows), rows)
        col = lanes(r, HEAD_SIZE)
        e = jnp.exp2(t[at] - jnp.max(peak[at], -1, keepdims=True))
        prob = e * (1.0 / jnp.sum(e, -1, keepdims=True))
        w = prob.astype(BF16)
        weights[at] = w
        o = dot(w, values[...], 1, 0).astype(BF16)
        o_all[:, col] = o
        row_dot = jnp.sum(dos[at].astype(F32) * o.astype(F32), -1, keepdims=True)
        ds = (prob * (dp[at] - row_dot)).astype(BF16)
        dscores[at] = ds
        dq_all[:, col] = (dot(ds, keys[...], 1, 0) * SCALE).astype(BF16)
        return carry

    lax.fori_loop(0, heads, finish, 0)
    puts = [pltpu.make_async_copy(src, dst, put_sem.at[i]) for i, (src, dst) in enumerate(((o_all, og), (dq_all, dqg)))]
    for copy in puts:
        copy.start()

    def gradients(low, count):
        at = slice(low, low + count)
        return dot(qs[...], dscores[:, at], 0, 0).T * SCALE, dot(dos[...], weights[:, at], 0, 0).T

    def make_terms(side, part):
        for i, g in enumerate(gradients(column(side, part), width)):
            for j in range(half):
                p = part * half + j
                b = block_of(side, p)
                value = g[j * BLK : (j + 1) * BLK]
                both = [jnp.where(b == block, value, 0.0) for block in (0, 1)]
                terms[side, p, i] = jnp.concatenate(both, 0).reshape(terms.shape[3:]).astype(BF16)

    rounds = []
    for step in range((me.right + 1) // 2):
        rounds.append([(w, reach[w] - 2 * step - i) for i in (0, 1) for w in (0, 1) if reach[w] - 2 * step - i > 0])
    rounds.append([(0, 0)])
    first, direct, second, flying = {}, {}, {}, {}

    def target(direction, far):
        return slot_of[far if direction == 0 else -far]

    def slots(r):
        return [target(*unit) for unit in rounds[r]] if r < len(rounds) else []

    def send_first(r):
        for p in slots(r):
            first[p] = go(
                remote(terms.at[FAR, p], relay_in.at[p], x_send.at[0, p], x_recv.at[0, p], me.x_peer(-1 if p % 2 else 1))
            )

    def send_direct(r):
        for p in slots(r):
            side, d = (RIGHT, 1) if p % 2 else (LEFT, -1)
            direct[p] = go(
                remote(terms.at[side, p], from_x.at[0, p], x_send.at[1, p], x_recv.at[1, p], me.x_peer(d))
            )

    def send_second(r):
        for p in slots(r):
            first[p].wait_recv()
            side = LEFT if p % 2 else RIGHT
            relay_out[p] = (relay_in[p].astype(F32) + terms[side, p].astype(F32)).astype(BF16)
        for p in slots(r):
            second[p] = go(
                remote(relay_out.at[p], from_x.at[1, p], x_send.at[2, p], x_recv.at[2, p], me.x_peer(-1 if p % 2 else 1))
            )

    def total(direction, far):
        p = target(direction, far)
        direct[p].wait_recv()
        second[p].wait_recv()
        value = terms[OWN, p].astype(F32) + from_x[0, p].astype(F32) + from_x[1, p].astype(F32)
        before = [(direction, far + 2)] if far else [(w, f) for f in (1, 2) for w in (0, 1)]
        for w, f in before:
            if f <= reach[w]:
                flying[w, f].wait_recv()
                value = value + ring_in[w, f].astype(F32)
        return value.astype(BF16)

    def send_ring(r):
        for direction, far in rounds[r]:
            ring_out[direction, far] = total(direction, far)
        for direction, far in rounds[r]:
            stride = min(2, far)
            flying[direction, far] = go(
                remote(
                    ring_out.at[direction, far], ring_in.at[direction, far],
                    z_send.at[direction, far], z_recv.at[direction, far],
                    me.z_peer(stride if direction == 0 else -stride),
                )
            )

    def head_out(which, src_at, dst, size):
        copies = []
        for d in range(1, nh):
            copies.append(
                go(
                    remote(
                        src_at(me.wrap_head(d)), dst.at[:, lanes(mine, size)],
                        out_send.at[which, d], out_recv.at[which, d], me.head_peer(d),
                    )
                )
            )
        return copies

    results = []
    make_terms(FAR, 1)
    send_first(0)
    send_first(1)
    make_terms(RIGHT, 1)
    make_terms(LEFT, 1)
    send_direct(0)
    make_terms(OWN, 1)
    for copy in puts:
        copy.wait()
    mids = [
        pltpu.make_async_copy(og.at[token_rows(mine)], own_q, own_sem.at[0]),
        pltpu.make_async_copy(dqg.at[token_rows(mine)], own_do, own_sem.at[1]),
    ]
    for copy in mids:
        copy.start()
    for i, (src, dst) in enumerate(((og, o_out), (dqg, dq_out))):
        results += head_out(i, lambda j, src=src: src.at[token_rows(j)], dst, qw)
    for i, g in enumerate(gradients(0, span)):
        span_grad[i] = g[0:rows]
        other[i] = g[rows:span].astype(BF16)
    send_second(0)
    send_direct(1)
    pair = [
        go(remote(other.at[i], pair_in.at[i], pair_send.at[i], pair_recv.at[i], me.partner(mine))) for i in (0, 1)
    ]
    make_terms(FAR, 0)
    send_first(2)
    make_terms(RIGHT, 0)
    make_terms(LEFT, 0)
    send_second(1)
    send_direct(2)
    send_first(3)
    send_ring(0)
    make_terms(OWN, 0)
    for copy in mids:
        copy.wait()
    mids = [
        pltpu.make_async_copy(own_q, o_out.at[:, lanes(mine, qw)], own_sem.at[0]),
        pltpu.make_async_copy(own_do, dq_out.at[:, lanes(mine, qw)], own_sem.at[1]),
    ]
    for copy in mids:
        copy.start()
    for i in (0, 1):
        pair[i].wait_recv()
        noisy_sum[i] = (span_grad[i] + pair_in[i].astype(F32)).astype(BF16)
    put = pltpu.make_async_copy(noisy_sum, ng, put_sem.at[0])
    put.start()
    for r in range(1, len(rounds)):
        if r > 1:
            send_direct(r + 1)
            send_first(r + 2)
        if r + 1 < len(rounds) or r == 1:
            send_second(r + 1)
        if r == len(rounds) - 1:
            break
        send_ring(r)
        if r == 1:
            put.wait()
            tail = [pltpu.make_async_copy(ng.at[i, token_rows(mine)], ref, own_sem.at[2 + i]) for i, ref in enumerate((own_k, own_v))]
            for copy in tail:
                copy.start()
            for i, dst in enumerate((dk_out, dv_out)):
                results += head_out(2 + i, lambda j, i=i: ng.at[i, token_rows(j)], dst, kw)
            for copy in tail:
                copy.wait()
            for i, (ref, dst) in enumerate(((own_k, dk_out), (own_v, dv_out))):
                mids.append(pltpu.make_async_copy(ref, dst.at[:, lanes(mine, kw)], own_sem.at[2 + i]))
                mids[-1].start()
    final[...] = total(0, 0)
    for i, dst in enumerate((dck_out, dcv_out)):
        results += head_out(4 + i, lambda j, i=i: final.at[i, j], dst, kw)
        mids.append(pltpu.make_async_copy(final.at[i, mine], dst.at[:, lanes(mine, kw)], own_sem.at[4 + i]))
        mids[-1].start()
    for copy in results:
        copy.wait_recv()
    for copy in sends:
        copy.wait_send()
    for copy in mids:
        copy.wait()


def everything(nz, nh, listed, q, do, k, v, ck, cv):
    few, qw, kw, crows = q.shape[0], q.shape[1] // nh, k.shape[1] // nh, ck.shape[0]
    rows = few * nh
    span = 2 * rows
    count = span + NX * nz * BLK
    stacked = rows * (qw // HEAD_SIZE)
    half = nz // 2
    unit = (2, nh, crows, kw)
    dma = pltpu.SemaphoreType.DMA

    def shape(*dims):
        return jax.ShapeDtypeStruct(dims, BF16)

    return pl.pallas_call(
        functools.partial(kernel, nz, nh),
        out_shape=(
            shape(few, nh * qw), shape(few, nh * qw), shape(few, nh * kw), shape(few, nh * kw),
            shape(crows, nh * kw), shape(crows, nh * kw),
            shape(rows, qw), shape(rows, qw), shape(span, kw), shape(span, kw),
            shape(rows, qw), shape(rows, qw), shape(2, rows, kw),
        ),
        in_specs=[SMEM] + [ANY] * 6,
        out_specs=(ANY,) * 13,
        scratch_shapes=[
            pltpu.VMEM((NX, nz) + unit, BF16),
            pltpu.VMEM((few, qw), BF16),
            pltpu.VMEM((few, qw), BF16),
            pltpu.VMEM((few, kw), BF16),
            pltpu.VMEM((few, kw), BF16),
            pltpu.VMEM((rows, qw), BF16),
            pltpu.VMEM((rows, qw), BF16),
            pltpu.VMEM((rows, qw), BF16),
            pltpu.VMEM((rows, qw), BF16),
            pltpu.VMEM((stacked, kw), BF16),
            pltpu.VMEM((stacked, kw), BF16),
            pltpu.VMEM((count, kw), BF16),
            pltpu.VMEM((count, kw), BF16),
            pltpu.VMEM((stacked, count), F32),
            pltpu.VMEM((stacked, count), F32),
            pltpu.VMEM((stacked, HEAD_SIZE), F32),
            pltpu.VMEM((stacked, count), BF16),
            pltpu.VMEM((stacked, count), BF16),
            pltpu.VMEM((1, count), F32),
            pltpu.VMEM((NX, nz) + unit, BF16),
            pltpu.VMEM((nz,) + unit, BF16),
            pltpu.VMEM((nz,) + unit, BF16),
            pltpu.VMEM((2, nz) + unit, BF16),
            pltpu.VMEM((2, half + 1) + unit, BF16),
            pltpu.VMEM((2, half + 1) + unit, BF16),
            pltpu.VMEM((2, rows, kw), BF16),
            pltpu.VMEM((2, rows, kw), BF16),
            pltpu.VMEM((2, rows, kw), F32),
            pltpu.VMEM((2, rows, kw), BF16),
            pltpu.VMEM(unit, BF16),
            dma((8, nh)), dma((8, nh)), dma((6,)), dma((4,)),
            dma((2, half + 1)), dma((2, half + 1)), dma((3, nz)), dma((3, nz)),
            dma((6, nh)), dma((6, nh)), dma((2,)), dma((2,)), dma((2,)),
            dma((3, nz)), dma((3, nz)), dma((2, half + 1)), dma((2, half + 1)),
        ],
        compiler_params=pltpu.CompilerParams(
            collective_id=0, has_side_effects=True, vmem_limit_bytes=60 * 2**20
        ),
        name="everything",
    )(listed, q, do, k, v, ck, cv)


def settle_kernel(*refs):
    count = len(refs) // 3
    ins, outs, held = refs[:count], refs[count : 2 * count], refs[2 * count : 3 * count]
    sem = refs[3 * count]
    loads = [pltpu.make_async_copy(a, b, sem.at[0, i]) for i, (a, b) in enumerate(zip(ins, held))]
    stores = [pltpu.make_async_copy(a, b, sem.at[1, i]) for i, (a, b) in enumerate(zip(held, outs))]
    for copy in loads:
        copy.start()
    for load, store in zip(loads, stores):
        load.wait()
        store.start()
    for copy in stores:
        copy.wait()


def settle(arrays):
    shapes = [(a.shape, a.dtype) for a in arrays]
    return pl.pallas_call(
        settle_kernel,
        out_shape=tuple(jax.ShapeDtypeStruct(*s) for s in shapes),
        in_specs=[ANY] * len(arrays),
        out_specs=(ANY,) * len(arrays),
        scratch_shapes=[pltpu.VMEM(*s) for s in shapes]
        + [pltpu.SemaphoreType.DMA((2, len(arrays)))] ,
        name="settle",
    )(*arrays)


def shards(nz, nh, queries, nk, nv, ck, cv, output_gradient, history_list):
    listed = lax.dynamic_index_in_dim(history_list, lax.axis_index("ctx"), 0, keepdims=False)
    results = everything(nz, nh, listed, queries, output_gradient, nk, nv, ck, cv)
    return settle(results[:6])


def solution(mesh):
    nz, nh = mesh.shape["ctx"] // NX, mesh.shape["head"]
    tokens = P(("ctx", "head"), None)
    return jax.shard_map(
        functools.partial(shards, nz, nh),
        mesh=mesh,
        in_specs=(tokens,) * 6 + (P(),),
        out_specs=(tokens,) * 6,
        check_vma=False,
    )
```

time: 410 us -> 96.7 us (0.24)
  waiting for transfers between devices: 103 us -> 0 us
  Pallas kernels: 0 us -> 94.5 us
  starting transfers between devices: 93.5 us -> 0 us
  blocking collectives: 90.9 us -> 0 us
  local copies, waits for them, and re-layouts: 61.5 us -> 1.27 us
  matrix products: 41.9 us -> 0 us
  other arithmetic: 15.4 us -> 0 us
    pallas_call x0 -> x2, Pallas kernels: none -> 94.5 us  [the longest x1 92.6 us: everything(): pl.pallas_call(functools.partial(kernel, nz, nh), out_shape=(shape(few, n...]
    all_to_all x3 -> x0, blocking collectives: 90.9 us -> none  [the longest x1 65.3 us: shards(): lax.all_to_all(slot_key_grads, 'ctx', split_axis=0, concat_axis=0, tiled=...]
    all_to_all x13 -> x0, waiting for transfers between devices: 90.3 us -> none  [the longest x1 48.1 us: shards(): lax.all_to_all(slot_value_grads, 'ctx', split_axis=0, concat_axis=0, tile...]
    all_to_all x13 -> x0, starting transfers between devices: 82.8 us -> none  [the longest x1 14.2 us: shards(): lax.all_to_all(send_keys, 'ctx', split_axis=0, concat_axis=0, tiled=True)]
    dot_general x36 -> x0, matrix products: 41.9 us -> none  [the longest x5 13.8 us: output_tile(): jnp.einsum('gqrk,kgd->qgrd', softmax_weights, tile_values, preferred_elem...]
    ppermute x4 -> x0, waiting for transfers between devices: 12.7 us -> none  [swapped(): return lax.ppermute(block, axis, route)]
    dynamic_slice x28 -> x0, local copies, waits for them, and re-layouts: 12.4 us -> none  [the longest x12 5.74 us: clean_tile(): lax.dynamic_slice_in_dim(live_slots, first_slot, slot_group, 0)]
    reshape x14 -> x0, local copies, waits for them, and re-layouts: 11 us -> none  [the longest x12 10.3 us: clean_tile(): jnp.repeat(lax.dynamic_slice_in_dim(live_slots, first_slot, slot_group, 0...]
  transfers between devices with their start and end apart: 17 -> 0, of which waited for: 13 -> 0; matrix products, arithmetic and copies ran while one was open for 27% -> 0% of each run, Pallas kernels for 0% -> 0%
where the time goes in v2:
time: 96.7 us; the launch traced here: 96.5 us
  Pallas kernels  94.5 us (98%)
  local copies, waits for them, and re-layouts  1.27 us (1%)
    pallas_call x1, Pallas kernels, everything(): pl.pallas_call(functools.partial(kernel, nz, nh), out_shape=(shape(few, n...  92.6 us

profile of v2, /device:TPU:1, one launch (start us, length us, event | category | flops | bytes accessed | tf_op | source)
XLA Modules:
  0.0 96.5 jit_solution(9483858934981783734)
XLA Ops:
  0.6 0.0 copy-start
  0.7 0.7 copy-done
  1.4 0.5 dynamic-slice_bitcast_fusion.listed
  1.9 92.6 %everything.1 = (bf16[24,6144]{1,0:T(8,128)(2,1)}, bf16[24,6144]{1,0:T(8,128)(2,1)}, bf16[24,1024]{1,0:T(8,128)(2,1)}, bf16[24,1024]{1,0:T(8,128)(2,1)}, bf16[8,...) custom-call(s32[64]{0:T(128)} %dynamic-slice_bitcast_fusion.listed, ...), custom_call_target="tpu_custom_call" | custom-call | tf_op jit(solution)/shard_map/everything/pallas_call | solution.py:519
  94.5 1.9 %settle.1 = (bf16[24,6144]{1,0:T(8,128)(2,1)}, bf16[24,6144]{1,0:T(8,128)(2,1)}, bf16[24,1024]{1,0:T(8,128)(2,1)}, bf16[24,1024]{1,0:T(8,128)(2,1)}, bf16[8,1024]{1,0:T(8,128)(2,1)}, /*index=5*/bf16[8,1024]{1,0:T(8,128)(2,1)}) custom-call(bf16[24,6144]{1,0:T(8,128)(2,1)} %get-tuple-element.12.refs_0_, bf16[24,6144]{1,0:T(8,128)(2,1)} %get-tuple-element.13.refs_1_, ...), custom_call_target="tpu_custom_call" | custom-call | tf_op jit(solution)/shard_map/settle/pallas_call | solution.py:589
Async XLA Ops:
  0.6 0.8 copy-start

commit v3 on v2

--- a/solution.py
+++ b/solution.py
@@ -87,12 +87,12 @@
 
 
 def kernel(
-    nz, nh, listed, q, do, k, v, ck, cv,
-    o_out, dq_out, dk_out, dv_out, dck_out, dcv_out, qg, dog, kn, vn, og, dqg, ng,
-    kv, own_q, own_do, own_k, own_v, q_all, do_all, o_all, dq_all, qs, dos, keys, values,
-    t, dp, peak, weights, dscores, bias, terms, relay_in, relay_out, from_x, ring_in, ring_out,
+    nz, nh, history, q, do, k, v, ck, cv,
+    o_out, dq_out, dk_out, dv_out, dck_out, dcv_out, qg, dog, kn, vn, og, dqg, ng, kp, vp,
+    listed, kv, own_q, own_do, own_k, own_v, own_kp, own_vp, q_all, do_all, o_all, dq_all, qs, dos, keys, values,
+    t, dp, tops, peak, norm, acc, weights, dscores, bias, terms, relay_in, relay_out, direct_in, second_in, ring_in, ring_out,
     other, pair_in, span_grad, noisy_sum, final,
-    in_send, in_recv, own_sem, load_sem, gz_send, gz_recv, gx_send, gx_recv,
+    list_sem, in_send, in_recv, own_sem, load_sem, gz_send, gz_recv, gx_send, gx_recv,
     out_send, out_recv, put_sem, pair_send, pair_recv, x_send, x_recv, z_send, z_recv,
 ):
     me = Place(nz, nh)
@@ -119,6 +119,9 @@
     def token_rows(index):
         return pl.ds(pl.multiple_of(index * few, 8), few)
 
+    ctx = lax.axis_index("ctx")
+    listing = pltpu.make_async_copy(history, listed, list_sem)
+    listing.start()
     local = [
         pltpu.make_async_copy(ck.at[:, lanes(mine, kw)], kv.at[OWN, 0, 0, mine], own_sem.at[0]),
         pltpu.make_async_copy(cv.at[:, lanes(mine, kw)], kv.at[OWN, 0, 1, mine], own_sem.at[1]),
@@ -147,7 +150,11 @@
     clean = [spread(i, src, lambda j, i=i: kv.at[OWN, 0, i, j], kw) for i, src in enumerate((ck, cv))]
     noisy = [spread(2 + i, src, lambda j, dst=dst: dst.at[token_rows(j)], kw) for i, (src, dst) in enumerate(((k, kn), (v, vn)))]
     wide = [spread(4 + i, src, lambda j, dst=dst: dst.at[token_rows(j)], qw) for i, (src, dst) in enumerate(((q, qg), (do, dog)))]
-    for copy in local[:2] :
+    pair_kv = [
+        go(remote(src, dst, in_send.at[6 + i, 0], in_recv.at[6 + i, 0], me.partner(mine)))
+        for i, (src, dst) in enumerate(((k, kp), (v, vp)))
+    ]
+    for copy in local[:2]:
         copy.wait()
     for copy in sum(clean, []):
         copy.wait_recv()
@@ -157,11 +164,11 @@
     def source(direction, far):
         return slot_of[-far if direction == 0 else far]
 
-    def hop(direction, far, stride):
-        arriving[direction, far + stride] = go(
+    def hop(direction, far, stride, i):
+        arriving[direction, far + stride, i] = go(
             remote(
-                kv.at[OWN, source(direction, far)], kv.at[OWN, source(direction, far + stride)],
-                gz_send.at[direction, far + stride], gz_recv.at[direction, far + stride],
+                kv.at[OWN, source(direction, far), i], kv.at[OWN, source(direction, far + stride), i],
+                gz_send.at[direction, far + stride, i], gz_recv.at[direction, far + stride, i],
                 me.z_peer(stride if direction == 0 else -stride),
             )
         )
@@ -179,29 +186,42 @@
         across[p] = go(remote(kv.at[side, p], kv.at[FAR, p], gx_send.at[2, p], gx_recv.at[2, p], me.x_peer(d)))
 
     def block_of(side, p):
-        return listed[me.wrap_x(SIDES[side]) * nz + me.wrap_z(offsets[p])]
+        return listed[ctx, me.wrap_x(SIDES[side]) * nz + me.wrap_z(offsets[p])]
 
     def column(side, part):
         return span + side * nz * BLK + part * width
 
-    def score(low, count):
+    chunks = [(0, span)] + [(column(side, part), width) for side in range(NX) for part in (0, 1)]
+
+    def score(index):
+        low, count = chunks[index]
         kk, vv = keys[low : low + count], values[low : low + count]
-
-        def body(r, carry):
-            at = pl.ds(pl.multiple_of(r * rows, rows), rows)
-            s = dot(qs[at], kk, 1, 1) * (SCALE * LOG2E) + bias[:, low : low + count]
-            t[at, low : low + count] = s
+        for r in range(heads):
+            at = slice(r * rows, (r + 1) * rows)
+            s = dot(qs[at], kk, 1, 1) * (SCALE * LOG2E)
+            if index:
+                s = s + bias[:, low : low + count]
+            groups = [s[:, j : j + HEAD_SIZE] for j in range(0, count, HEAD_SIZE)]
+            most = jnp.max(functools.reduce(jnp.maximum, groups), -1, keepdims=True)
+            if index:
+                old = peak[at]
+                top = jnp.maximum(old, most)
+            else:
+                top = jnp.broadcast_to(most, (rows, HEAD_SIZE))
+            groups = [jnp.exp2(g - top) for g in groups]
+            for j, g in enumerate(groups):
+                t[at, low + j * HEAD_SIZE : low + (j + 1) * HEAD_SIZE] = g
+            tops[index, at] = top
+            peak[at] = top
+            mass = functools.reduce(jnp.add, groups)
+            part = dot(jnp.concatenate(groups, 1).astype(BF16), vv, 1, 0)
+            if index:
+                shrink = jnp.exp2(old - top)
+                mass = mass + norm[at] * shrink
+                part = part + acc[at] * shrink
+            norm[at] = mass
+            acc[at] = part
             dp[at, low : low + count] = dot(dos[at], vv, 1, 1)
-            top = peak[at]
-            if count % HEAD_SIZE:
-                top = jnp.maximum(top, jnp.max(s, -1, keepdims=True))
-            else:
-                for j in range(0, count, HEAD_SIZE):
-                    top = jnp.maximum(top, s[:, j : j + HEAD_SIZE])
-            peak[at] = top
-            return carry
-
-        lax.fori_loop(0, heads, body, 0)
 
     def score_clean(side, part):
         low = column(side, part)
@@ -215,122 +235,124 @@
                 dst[low + j * BLK : low + (j + 1) * BLK] = jnp.where(b == 1, both[BLK:], both[:BLK]).astype(BF16)
             dead = jnp.where(place == j, jnp.where(b < 0, -1e30, 0.0), dead)
         bias[:, low : low + width] = dead
-        score(low, width)
-
-    def score_noisy():
-        for copy in back + loads:
+        score(1 + 2 * side + part)
+
+    def take_rows():
+        for copy in sum(noisy + other_noisy, []) + sum(wide, []):
+            copy.wait_recv()
+        for copy in back:
             copy.wait()
-        for copy in pair_kv:
-            copy.wait_recv()
-        pulls = [pltpu.make_async_copy(src, dst.at[0:span], load_sem.at[2 + i]) for i, (src, dst) in enumerate(((kn, keys), (vn, values)))]
+        pulls = [
+            pltpu.make_async_copy(src, dst, load_sem.at[i])
+            for i, (src, dst) in enumerate(
+                ((qg, q_all), (dog, do_all), (kn, keys.at[0:span]), (vn, values.at[0:span]))
+            )
+        ]
         for copy in pulls:
             copy.start()
+        for copy in pulls:
+            copy.wait()
         for r in range(heads):
             at, col = slice(r * rows, (r + 1) * rows), slice(r * HEAD_SIZE, (r + 1) * HEAD_SIZE)
             qs[at] = q_all[:, col]
             dos[at] = do_all[:, col]
-        bias[:, 0:span] = jnp.zeros((1, span), F32)
-        peak[...] = jnp.full(peak.shape, -3e38, F32)
-        for copy in pulls:
-            copy.wait()
-        score(0, span)
 
     rounds = [[(0, 0)]]
     for near in range(1, me.right + 1, 2):
-        rounds.append([(w, far) for far in (near, near + 1) for w in (0, 1) if far <= reach[w]])
+        rounds.append([(w, far) for far in (near + 1, near) for w in (0, 1) if far <= reach[w]])
 
     def advance(r):
-        for direction, far in rounds[r]:
-            if r == 0:
-                for stride in (1, 2):
+        if r == 0:
+            for stride in (2, 1):
+                for i in (0, 1):
                     for w in (0, 1):
                         if stride <= reach[w]:
-                            hop(w, 0, stride)
-            else:
-                arriving[direction, far].wait_recv()
-                if far + 2 <= reach[direction]:
-                    hop(direction, far, 2)
-            pass_on(source(direction, far))
+                            hop(w, 0, stride, i)
+            pass_on(source(0, 0))
+            return
+        for begin in range(0, len(rounds[r]), 2):
+            group = rounds[r][begin : begin + 2]
+            for i in (0, 1):
+                for direction, far in group:
+                    arriving[direction, far, i].wait_recv()
+                    if far + 2 <= reach[direction]:
+                        hop(direction, far, 2, i)
+            for unit in group:
+                pass_on(source(*unit))
 
     def hand_round(r):
         for unit in rounds[r]:
             hand_over(source(*unit))
 
-    last = len(rounds) - 1
-    for r in range(last + 1):
-        advance(r)
-        if r == min(1, last):
-            for copy in local[2:]:
-                copy.wait()
-            back = [
-                pltpu.make_async_copy(src, dst.at[token_rows(mine)], own_sem.at[i])
-                for i, (src, dst) in enumerate(((own_k, kn), (own_v, vn), (own_q, qg), (own_do, dog)))
-            ]
-            for copy in back:
-                copy.start()
-        if r == min(2, last):
-            for copy in sum(noisy, []):
-                copy.wait_recv()
-            for copy in back:
-                copy.wait()
-            back = []
-            pair_kv = [
-                go(
-                    remote(
-                        ref.at[0:rows], ref.at[rows:span], in_send.at[6 + i, 0], in_recv.at[6 + i, 0],
-                        me.partner(mine),
-                    )
-                )
-                for i, ref in enumerate((kn, vn))
-            ]
-            for copy in sum(wide, []):
-                copy.wait_recv()
-            loads = [pltpu.make_async_copy(src, dst, load_sem.at[i]) for i, (src, dst) in enumerate(((qg, q_all), (dog, do_all)))]
-            for copy in loads:
-                copy.start()
-        if r >= 2:
-            hand_round(r - 2)
-        if r == max(last - 1, min(2, last)):
-            score_noisy()
-            if last > 2:
-                score_clean(OWN, 0)
-    if last <= 2:
-        score_clean(OWN, 0)
-    if last > 0:
-        hand_round(last - 1)
+    advance(0)
+    for copy in pair_kv:
+        copy.wait_recv()
+    other_noisy = [
+        spread(6 + i, src, lambda j, dst=dst: dst.at[pl.ds(pl.multiple_of(rows + j * few, 8), few)], kw)
+        for i, (src, dst) in enumerate(((kp, kn), (vp, vn)))
+    ]
+    for i, (src, dst) in enumerate(((kp, own_kp), (vp, own_vp))):
+        local.append(pltpu.make_async_copy(src.at[:, lanes(mine, kw)], dst, own_sem.at[6 + i]))
+        local[-1].start()
+    advance(1)
+    for copy in local[2:]:
+        copy.wait()
+    back = [
+        pltpu.make_async_copy(src, dst, own_sem.at[i])
+        for i, (src, dst) in enumerate(
+            (
+                (own_k, kn.at[token_rows(mine)]),
+                (own_v, vn.at[token_rows(mine)]),
+                (own_q, qg.at[token_rows(mine)]),
+                (own_do, dog.at[token_rows(mine)]),
+                (own_kp, kn.at[pl.ds(pl.multiple_of(rows + mine * few, 8), few)]),
+                (own_vp, vn.at[pl.ds(pl.multiple_of(rows + mine * few, 8), few)]),
+            )
+        )
+    ]
+    for copy in back:
+        copy.start()
+    listing.wait()
+    take_rows()
+    advance(2)
+    hand_round(0)
+    score(0)
+    hand_round(1)
+    score_clean(OWN, 0)
+    advance(3)
+    hand_round(2)
+    score_clean(RIGHT, 0)
+    advance(4)
+    score_clean(LEFT, 0)
+    hand_round(3)
     score_clean(OWN, 1)
-    done = sum(len(units) for units in rounds[:last])
-    early = done >= half
-    if early:
-        score_clean(RIGHT, 0)
-        score_clean(LEFT, 0)
-    hand_round(last)
-    if not early:
-        score_clean(RIGHT, 0)
-        score_clean(LEFT, 0)
+    for p in range(half):
+        across[p].wait_recv()
+    score_clean(FAR, 0)
+    hand_round(4)
     score_clean(RIGHT, 1)
     score_clean(LEFT, 1)
-    for part in (0, 1):
-        for p in range(part * half, (part + 1) * half):
-            across[p].wait_recv()
-        score_clean(FAR, part)
-
-    def finish(r, carry):
-        at = pl.ds(pl.multiple_of(r * rows, rows), rows)
-        col = lanes(r, HEAD_SIZE)
-        e = jnp.exp2(t[at] - jnp.max(peak[at], -1, keepdims=True))
-        prob = e * (1.0 / jnp.sum(e, -1, keepdims=True))
-        w = prob.astype(BF16)
-        weights[at] = w
-        o = dot(w, values[...], 1, 0).astype(BF16)
+    for p in range(half, nz):
+        across[p].wait_recv()
+    score_clean(FAR, 1)
+
+    def finish(r):
+        at = slice(r * rows, (r + 1) * rows)
+        col = slice(r * HEAD_SIZE, (r + 1) * HEAD_SIZE)
+        top, inverse = peak[at], 1.0 / jnp.sum(norm[at], -1, keepdims=True)
+        o = (acc[at] * inverse).astype(BF16)
         o_all[:, col] = o
         row_dot = jnp.sum(dos[at].astype(F32) * o.astype(F32), -1, keepdims=True)
-        ds = (prob * (dp[at] - row_dot)).astype(BF16)
-        dscores[at] = ds
-        dq_all[:, col] = (dot(ds, keys[...], 1, 0) * SCALE).astype(BF16)
-        return carry
-
-    lax.fori_loop(0, heads, finish, 0)
+        for index, (low, count) in enumerate(chunks):
+            factor = jnp.exp2(tops[index, at] - top) * inverse
+            for j in range(low, low + count, HEAD_SIZE):
+                prob = t[at, j : j + HEAD_SIZE] * factor
+                weights[at, j : j + HEAD_SIZE] = prob.astype(BF16)
+                dscores[at, j : j + HEAD_SIZE] = (prob * (dp[at, j : j + HEAD_SIZE] - row_dot)).astype(BF16)
+        dq_all[:, col] = (dot(dscores[at], keys[...], 1, 0) * SCALE).astype(BF16)
+
+    for r in range(heads):
+        finish(r)
     puts = [pltpu.make_async_copy(src, dst, put_sem.at[i]) for i, (src, dst) in enumerate(((o_all, og), (dq_all, dqg)))]
     for copy in puts:
         copy.start()
@@ -342,11 +364,12 @@
     def make_terms(side, part):
         for i, g in enumerate(gradients(column(side, part), width)):
             for j in range(half):
-                p = part * half + j
-                b = block_of(side, p)
-                value = g[j * BLK : (j + 1) * BLK]
-                both = [jnp.where(b == block, value, 0.0) for block in (0, 1)]
-                terms[side, p, i] = jnp.concatenate(both, 0).reshape(terms.shape[3:]).astype(BF16)
+                terms[side, part * half + j, i] = g[j * BLK : (j + 1) * BLK].astype(BF16)
+
+    def placed(value, whose, side, p):
+        b = listed[me.wrap_x(whose) * nz + me.z, me.wrap_x(SIDES[side]) * nz + me.wrap_z(offsets[p])]
+        value = value.astype(F32)
+        return jnp.concatenate([jnp.where(b == block, value, 0.0) for block in (0, 1)], 0)
 
     rounds = []
     for step in range((me.right + 1) // 2):
@@ -370,43 +393,56 @@
         for p in slots(r):
             side, d = (RIGHT, 1) if p % 2 else (LEFT, -1)
             direct[p] = go(
-                remote(terms.at[side, p], from_x.at[0, p], x_send.at[1, p], x_recv.at[1, p], me.x_peer(d))
+                remote(terms.at[side, p], direct_in.at[p], x_send.at[1, p], x_recv.at[1, p], me.x_peer(d))
             )
 
     def send_second(r):
-        for p in slots(r):
-            first[p].wait_recv()
-            side = LEFT if p % 2 else RIGHT
-            relay_out[p] = (relay_in[p].astype(F32) + terms[side, p].astype(F32)).astype(BF16)
-        for p in slots(r):
-            second[p] = go(
-                remote(relay_out.at[p], from_x.at[1, p], x_send.at[2, p], x_recv.at[2, p], me.x_peer(-1 if p % 2 else 1))
-            )
-
-    def total(direction, far):
+        for begin in (0, 2):
+            group = slots(r)[begin : begin + 2]
+            for p in group:
+                first[p].wait_recv()
+                side = LEFT if p % 2 else RIGHT
+                for i in (0, 1):
+                    relay_out[p, i] = (
+                        placed(relay_in[p, i], 1 if p % 2 else -1, side, p) + placed(terms[side, p, i], 0, side, p)
+                    ).astype(BF16)
+            for p in group:
+                second[p] = go(
+                    remote(relay_out.at[p], second_in.at[p], x_send.at[2, p], x_recv.at[2, p], me.x_peer(-1 if p % 2 else 1))
+                )
+
+    def total(direction, far, i):
         p = target(direction, far)
-        direct[p].wait_recv()
-        second[p].wait_recv()
-        value = terms[OWN, p].astype(F32) + from_x[0, p].astype(F32) + from_x[1, p].astype(F32)
+        if i == 0:
+            direct[p].wait_recv()
+            second[p].wait_recv()
+        value = (
+            placed(terms[OWN, p, i], 0, OWN, p)
+            + placed(direct_in[p, i], -1 if p % 2 else 1, OWN, p)
+            + second_in[p, i].astype(F32)
+        )
         before = [(direction, far + 2)] if far else [(w, f) for f in (1, 2) for w in (0, 1)]
         for w, f in before:
             if f <= reach[w]:
-                flying[w, f].wait_recv()
-                value = value + ring_in[w, f].astype(F32)
+                flying[w, f, i].wait_recv()
+                value = value + ring_in[w, f, i].astype(F32)
         return value.astype(BF16)
 
     def send_ring(r):
-        for direction, far in rounds[r]:
-            ring_out[direction, far] = total(direction, far)
-        for direction, far in rounds[r]:
-            stride = min(2, far)
-            flying[direction, far] = go(
-                remote(
-                    ring_out.at[direction, far], ring_in.at[direction, far],
-                    z_send.at[direction, far], z_recv.at[direction, far],
-                    me.z_peer(stride if direction == 0 else -stride),
-                )
-            )
+        for begin in range(0, len(rounds[r]), 2):
+            group = rounds[r][begin : begin + 2]
+            for i in (0, 1):
+                for direction, far in group:
+                    ring_out[direction, far, i] = total(direction, far, i)
+                for direction, far in group:
+                    stride = min(2, far)
+                    flying[direction, far, i] = go(
+                        remote(
+                            ring_out.at[direction, far, i], ring_in.at[direction, far, i],
+                            z_send.at[direction, far, i], z_recv.at[direction, far, i],
+                            me.z_peer(stride if direction == 0 else -stride),
+                        )
+                    )
 
     def head_out(which, src_at, dst, size):
         copies = []
@@ -490,7 +526,8 @@
             for i, (ref, dst) in enumerate(((own_k, dk_out), (own_v, dv_out))):
                 mids.append(pltpu.make_async_copy(ref, dst.at[:, lanes(mine, kw)], own_sem.at[2 + i]))
                 mids[-1].start()
-    final[...] = total(0, 0)
+    for i, dst in enumerate((dck_out, dcv_out)):
+        final[i] = total(0, 0, i).astype(F32).reshape(final.shape[1:]).astype(BF16)
     for i, dst in enumerate((dck_out, dcv_out)):
         results += head_out(4 + i, lambda j, i=i: final.at[i, j], dst, kw)
         mids.append(pltpu.make_async_copy(final.at[i, mine], dst.at[:, lanes(mine, kw)], own_sem.at[4 + i]))
@@ -503,7 +540,7 @@
         copy.wait()
 
 
-def everything(nz, nh, listed, q, do, k, v, ck, cv):
+def everything(nz, nh, history, q, do, k, v, ck, cv):
     few, qw, kw, crows = q.shape[0], q.shape[1] // nh, k.shape[1] // nh, ck.shape[0]
     rows = few * nh
     span = 2 * rows
@@ -523,13 +560,17 @@
             shape(crows, nh * kw), shape(crows, nh * kw),
             shape(rows, qw), shape(rows, qw), shape(span, kw), shape(span, kw),
             shape(rows, qw), shape(rows, qw), shape(2, rows, kw),
+            shape(few, nh * kw), shape(few, nh * kw),
         ),
-        in_specs=[SMEM] + [ANY] * 6,
-        out_specs=(ANY,) * 13,
+        in_specs=[ANY] * 7,
+        out_specs=(ANY,) * 15,
         scratch_shapes=[
+            pltpu.SMEM(history.shape, jnp.int32),
             pltpu.VMEM((NX, nz) + unit, BF16),
             pltpu.VMEM((few, qw), BF16),
             pltpu.VMEM((few, qw), BF16),
+            pltpu.VMEM((few, kw), BF16),
+            pltpu.VMEM((few, kw), BF16),
             pltpu.VMEM((few, kw), BF16),
             pltpu.VMEM((few, kw), BF16),
             pltpu.VMEM((rows, qw), BF16),
@@ -542,31 +583,35 @@
             pltpu.VMEM((count, kw), BF16),
             pltpu.VMEM((stacked, count), F32),
             pltpu.VMEM((stacked, count), F32),
+            pltpu.VMEM((9, stacked, HEAD_SIZE), F32),
+            pltpu.VMEM((stacked, HEAD_SIZE), F32),
+            pltpu.VMEM((stacked, HEAD_SIZE), F32),
             pltpu.VMEM((stacked, HEAD_SIZE), F32),
             pltpu.VMEM((stacked, count), BF16),
             pltpu.VMEM((stacked, count), BF16),
             pltpu.VMEM((1, count), F32),
-            pltpu.VMEM((NX, nz) + unit, BF16),
-            pltpu.VMEM((nz,) + unit, BF16),
-            pltpu.VMEM((nz,) + unit, BF16),
-            pltpu.VMEM((2, nz) + unit, BF16),
-            pltpu.VMEM((2, half + 1) + unit, BF16),
-            pltpu.VMEM((2, half + 1) + unit, BF16),
+            pltpu.VMEM((NX, nz, 2, BLK, kw), BF16),
+            pltpu.VMEM((nz, 2, BLK, kw), BF16),
+            pltpu.VMEM((nz, 2, 2 * BLK, kw), BF16),
+            pltpu.VMEM((nz, 2, BLK, kw), BF16),
+            pltpu.VMEM((nz, 2, 2 * BLK, kw), BF16),
+            pltpu.VMEM((2, half + 1, 2, 2 * BLK, kw), BF16),
+            pltpu.VMEM((2, half + 1, 2, 2 * BLK, kw), BF16),
             pltpu.VMEM((2, rows, kw), BF16),
             pltpu.VMEM((2, rows, kw), BF16),
             pltpu.VMEM((2, rows, kw), F32),
             pltpu.VMEM((2, rows, kw), BF16),
             pltpu.VMEM(unit, BF16),
-            dma((8, nh)), dma((8, nh)), dma((6,)), dma((4,)),
-            dma((2, half + 1)), dma((2, half + 1)), dma((3, nz)), dma((3, nz)),
+            dma, dma((8, nh)), dma((8, nh)), dma((8,)), dma((4,)),
+            dma((2, half + 1, 2)), dma((2, half + 1, 2)), dma((3, nz)), dma((3, nz)),
             dma((6, nh)), dma((6, nh)), dma((2,)), dma((2,)), dma((2,)),
-            dma((3, nz)), dma((3, nz)), dma((2, half + 1)), dma((2, half + 1)),
+            dma((3, nz)), dma((3, nz)), dma((2, half + 1, 2)), dma((2, half + 1, 2)),
         ],
         compiler_params=pltpu.CompilerParams(
             collective_id=0, has_side_effects=True, vmem_limit_bytes=60 * 2**20
         ),
         name="everything",
-    )(listed, q, do, k, v, ck, cv)
+    )(history, q, do, k, v, ck, cv)
 
 
 def settle_kernel(*refs):
@@ -598,8 +643,7 @@
 
 
 def shards(nz, nh, queries, nk, nv, ck, cv, output_gradient, history_list):
-    listed = lax.dynamic_index_in_dim(history_list, lax.axis_index("ctx"), 0, keepdims=False)
-    results = everything(nz, nh, listed, queries, output_gradient, nk, nv, ck, cv)
+    results = everything(nz, nh, history_list, queries, output_gradient, nk, nv, ck, cv)
     return settle(results[:6])
 
 

time: 96.7 us -> 88.5 us (0.915)
  Pallas kernels: 94.5 us -> 87.4 us
  local copies, waits for them, and re-layouts: 1.27 us -> 0 us
    pallas_call x1, Pallas kernels: 92.6 us -> 85.5 us  [everything(): pl.pallas_call(functools.partial(kernel, nz, nh), out_shape=(shape(few, n...]
where the time goes in v3:
time: 88.5 us; the launch traced here: 88.2 us
  Pallas kernels  87.4 us (99%)
    pallas_call x1, Pallas kernels, everything(): pl.pallas_call(functools.partial(kernel, nz, nh), out_shape=(shape(few, n...  85.5 us
    pallas_call x1, Pallas kernels, settle(): pl.pallas_call(settle_kernel, out_shape=tuple((jax.ShapeDtypeStruct(*s) f...  1.91 us

profile of v3, /device:TPU:1, one launch (start us, length us, event | category | flops | bytes accessed | tf_op | source)
XLA Modules:
  0.0 88.2 jit_solution(17644264629575238349)
XLA Ops:
  0.6 85.5 %everything.1 = (bf16[24,6144]{1,0:T(8,128)(2,1)}, bf16[24,6144]{1,0:T(8,128)(2,1)}, bf16[24,1024]{1,0:T(8,128)(2,1)}, bf16[24,1024]{1,0:T(8,128)(2,1)}, bf16[8,...) custom-call(s32[64,64]{1,0:T(8,128)} %history.1, ...), custom_call_target="tpu_custom_call" | custom-call | tf_op jit(solution)/shard_map/everything/pallas_call | solution.py:556
  86.2 1.9 %settle.1 = (bf16[24,6144]{1,0:T(8,128)(2,1)}, bf16[24,6144]{1,0:T(8,128)(2,1)}, bf16[24,1024]{1,0:T(8,128)(2,1)}, bf16[24,1024]{1,0:T(8,128)(2,1)}, bf16[8,1024]{1,0:T(8,128)(2,1)}, /*index=5*/bf16[8,1024]{1,0:T(8,128)(2,1)}) custom-call(bf16[24,6144]{1,0:T(8,128)(2,1)} %get-tuple-element.12.refs_0_, bf16[24,6144]{1,0:T(8,128)(2,1)} %get-tuple-element.13.refs_1_, ...), custom_call_target="tpu_custom_call" | custom-call | tf_op jit(solution)/shard_map/settle/pallas_call | solution.py:634

commit v4 on v3

--- a/solution.py
+++ b/solution.py
@@ -90,7 +90,7 @@
     nz, nh, history, q, do, k, v, ck, cv,
     o_out, dq_out, dk_out, dv_out, dck_out, dcv_out, qg, dog, kn, vn, og, dqg, ng, kp, vp,
     listed, kv, own_q, own_do, own_k, own_v, own_kp, own_vp, q_all, do_all, o_all, dq_all, qs, dos, keys, values,
-    t, dp, tops, peak, norm, acc, weights, dscores, bias, terms, relay_in, relay_out, direct_in, second_in, ring_in, ring_out,
+    t, dp, tops, peak, norm, acc, weights, dscores, bias, terms, side_in, far_in, ring_in, ring_out,
     other, pair_in, span_grad, noisy_sum, final,
     list_sem, in_send, in_recv, own_sem, load_sem, gz_send, gz_recv, gx_send, gx_recv,
     out_send, out_recv, put_sem, pair_send, pair_recv, x_send, x_recv, z_send, z_recv,
@@ -132,7 +132,7 @@
     ]
     for copy in local:
         copy.start()
-    greet([me.head_peer(d) for d in range(1, nh)] + me.z_peers() + [me.x_peer(1), me.x_peer(-1)])
+    greet([me.head_peer(d) for d in range(1, nh)] + me.z_peers() + [me.x_peer(1), me.x_peer(-1), me.x_peer(2)])
 
     def spread(which, src, dst_at, size):
         copies = []
@@ -193,37 +193,45 @@
 
     chunks = [(0, span)] + [(column(side, part), width) for side in range(NX) for part in (0, 1)]
 
-    def score(index):
-        low, count = chunks[index]
-        kk, vv = keys[low : low + count], values[low : low + count]
+    batches = ((0, 1), (3, 5), (2, 7), (4, 6, 8))
+
+    def score(batch):
         for r in range(heads):
             at = slice(r * rows, (r + 1) * rows)
-            s = dot(qs[at], kk, 1, 1) * (SCALE * LOG2E)
-            if index:
-                s = s + bias[:, low : low + count]
-            groups = [s[:, j : j + HEAD_SIZE] for j in range(0, count, HEAD_SIZE)]
-            most = jnp.max(functools.reduce(jnp.maximum, groups), -1, keepdims=True)
-            if index:
+            groups = []
+            for index in batches[batch]:
+                low, count = chunks[index]
+                s = dot(qs[at], keys[low : low + count], 1, 1) * (SCALE * LOG2E)
+                if index:
+                    s = s + bias[:, low : low + count]
+                groups += [(low + j, s[:, j : j + HEAD_SIZE]) for j in range(0, count, HEAD_SIZE)]
+            most = jnp.max(functools.reduce(jnp.maximum, [g for _, g in groups]), -1, keepdims=True)
+            if batch:
                 old = peak[at]
                 top = jnp.maximum(old, most)
             else:
                 top = jnp.broadcast_to(most, (rows, HEAD_SIZE))
-            groups = [jnp.exp2(g - top) for g in groups]
-            for j, g in enumerate(groups):
-                t[at, low + j * HEAD_SIZE : low + (j + 1) * HEAD_SIZE] = g
-            tops[index, at] = top
+            groups = [(j, jnp.exp2(g - top)) for j, g in groups]
+            for j, g in groups:
+                t[at, j : j + HEAD_SIZE] = g
+            tops[batch, at] = top
             peak[at] = top
-            mass = functools.reduce(jnp.add, groups)
-            part = dot(jnp.concatenate(groups, 1).astype(BF16), vv, 1, 0)
-            if index:
+            mass = functools.reduce(jnp.add, [g for _, g in groups])
+            if batch:
                 shrink = jnp.exp2(old - top)
                 mass = mass + norm[at] * shrink
-                part = part + acc[at] * shrink
+                part = acc[at] * shrink
+            else:
+                part = jnp.zeros((rows, HEAD_SIZE), F32)
+            for index in batches[batch]:
+                low, count = chunks[index]
+                e = jnp.concatenate([g for j, g in groups if low <= j < low + count], 1).astype(BF16)
+                part = part + dot(e, values[low : low + count], 1, 0)
+                dp[at, low : low + count] = dot(dos[at], values[low : low + count], 1, 1)
             norm[at] = mass
             acc[at] = part
-            dp[at, low : low + count] = dot(dos[at], vv, 1, 1)
-
-    def score_clean(side, part):
+
+    def listed_rows(side, part):
         low = column(side, part)
         place = lax.broadcasted_iota(jnp.int32, (1, width), 1) // BLK
         dead = jnp.zeros((1, width), F32)
@@ -235,7 +243,6 @@
                 dst[low + j * BLK : low + (j + 1) * BLK] = jnp.where(b == 1, both[BLK:], both[:BLK]).astype(BF16)
             dead = jnp.where(place == j, jnp.where(b < 0, -1e30, 0.0), dead)
         bias[:, low : low + width] = dead
-        score(1 + 2 * side + part)
 
     def take_rows():
         for copy in sum(noisy + other_noisy, []) + sum(wide, []):
@@ -278,7 +285,12 @@
                     if far + 2 <= reach[direction]:
                         hop(direction, far, 2, i)
             for unit in group:
-                pass_on(source(*unit))
+                p = source(*unit)
+                pass_on(p)
+                if r == len(rounds) - 1:
+                    across[p] = go(
+                        remote(kv.at[OWN, p], kv.at[FAR, p], gx_send.at[2, p], gx_recv.at[2, p], me.x_peer(2))
+                    )
 
     def hand_round(r):
         for unit in rounds[r]:
@@ -316,25 +328,30 @@
     take_rows()
     advance(2)
     hand_round(0)
+    listed_rows(OWN, 0)
     score(0)
     hand_round(1)
-    score_clean(OWN, 0)
     advance(3)
     hand_round(2)
-    score_clean(RIGHT, 0)
+    listed_rows(RIGHT, 0)
+    listed_rows(LEFT, 0)
     advance(4)
-    score_clean(LEFT, 0)
+    score(1)
     hand_round(3)
-    score_clean(OWN, 1)
+    listed_rows(OWN, 1)
     for p in range(half):
         across[p].wait_recv()
-    score_clean(FAR, 0)
-    hand_round(4)
-    score_clean(RIGHT, 1)
-    score_clean(LEFT, 1)
+    listed_rows(FAR, 0)
+    score(2)
+    for unit in rounds[4]:
+        for i in (0, 1):
+            sideways[source(*unit), i].wait_recv()
+    listed_rows(RIGHT, 1)
+    listed_rows(LEFT, 1)
     for p in range(half, nz):
         across[p].wait_recv()
-    score_clean(FAR, 1)
+    listed_rows(FAR, 1)
+    score(3)
 
     def finish(r):
         at = slice(r * rows, (r + 1) * rows)
@@ -343,9 +360,9 @@
         o = (acc[at] * inverse).astype(BF16)
         o_all[:, col] = o
         row_dot = jnp.sum(dos[at].astype(F32) * o.astype(F32), -1, keepdims=True)
-        for index, (low, count) in enumerate(chunks):
-            factor = jnp.exp2(tops[index, at] - top) * inverse
-            for j in range(low, low + count, HEAD_SIZE):
+        for batch, indexes in enumerate(batches):
+            factor = jnp.exp2(tops[batch, at] - top) * inverse
+            for j in [j for low, count in (chunks[i] for i in indexes) for j in range(low, low + count, HEAD_SIZE)]:
                 prob = t[at, j : j + HEAD_SIZE] * factor
                 weights[at, j : j + HEAD_SIZE] = prob.astype(BF16)
                 dscores[at, j : j + HEAD_SIZE] = (prob * (dp[at, j : j + HEAD_SIZE] - row_dot)).astype(BF16)
@@ -366,8 +383,8 @@
             for j in range(half):
                 terms[side, part * half + j, i] = g[j * BLK : (j + 1) * BLK].astype(BF16)
 
-    def placed(value, whose, side, p):
-        b = listed[me.wrap_x(whose) * nz + me.z, me.wrap_x(SIDES[side]) * nz + me.wrap_z(offsets[p])]
+    def placed(value, whose, p):
+        b = listed[me.wrap_x(whose) * nz + me.z, me.x * nz + me.wrap_z(offsets[p])]
         value = value.astype(F32)
         return jnp.concatenate([jnp.where(b == block, value, 0.0) for block in (0, 1)], 0)
 
@@ -375,7 +392,7 @@
     for step in range((me.right + 1) // 2):
         rounds.append([(w, reach[w] - 2 * step - i) for i in (0, 1) for w in (0, 1) if reach[w] - 2 * step - i > 0])
     rounds.append([(0, 0)])
-    first, direct, second, flying = {}, {}, {}, {}
+    beside, opposite, flying = {}, {}, {}
 
     def target(direction, far):
         return slot_of[far if direction == 0 else -far]
@@ -383,43 +400,30 @@
     def slots(r):
         return [target(*unit) for unit in rounds[r]] if r < len(rounds) else []
 
-    def send_first(r):
+    def send_opposite(r):
         for p in slots(r):
-            first[p] = go(
-                remote(terms.at[FAR, p], relay_in.at[p], x_send.at[0, p], x_recv.at[0, p], me.x_peer(-1 if p % 2 else 1))
+            opposite[p] = go(
+                remote(terms.at[FAR, p], far_in.at[p], x_send.at[2, p], x_recv.at[2, p], me.x_peer(2))
             )
 
-    def send_direct(r):
+    def send_beside(r):
         for p in slots(r):
-            side, d = (RIGHT, 1) if p % 2 else (LEFT, -1)
-            direct[p] = go(
-                remote(terms.at[side, p], direct_in.at[p], x_send.at[1, p], x_recv.at[1, p], me.x_peer(d))
-            )
-
-    def send_second(r):
-        for begin in (0, 2):
-            group = slots(r)[begin : begin + 2]
-            for p in group:
-                first[p].wait_recv()
-                side = LEFT if p % 2 else RIGHT
-                for i in (0, 1):
-                    relay_out[p, i] = (
-                        placed(relay_in[p, i], 1 if p % 2 else -1, side, p) + placed(terms[side, p, i], 0, side, p)
-                    ).astype(BF16)
-            for p in group:
-                second[p] = go(
-                    remote(relay_out.at[p], second_in.at[p], x_send.at[2, p], x_recv.at[2, p], me.x_peer(-1 if p % 2 else 1))
+            for i, (side, d) in enumerate(((RIGHT, 1), (LEFT, -1))):
+                beside[p, i] = go(
+                    remote(terms.at[side, p], side_in.at[i, p], x_send.at[i, p], x_recv.at[i, p], me.x_peer(d))
                 )
 
     def total(direction, far, i):
         p = target(direction, far)
         if i == 0:
-            direct[p].wait_recv()
-            second[p].wait_recv()
+            beside[p, 0].wait_recv()
+            beside[p, 1].wait_recv()
+            opposite[p].wait_recv()
         value = (
-            placed(terms[OWN, p, i], 0, OWN, p)
-            + placed(direct_in[p, i], -1 if p % 2 else 1, OWN, p)
-            + second_in[p, i].astype(F32)
+            placed(terms[OWN, p, i], 0, p)
+            + placed(side_in[0, p, i], -1, p)
+            + placed(side_in[1, p, i], 1, p)
+            + placed(far_in[p, i], 2, p)
         )
         before = [(direction, far + 2)] if far else [(w, f) for f in (1, 2) for w in (0, 1)]
         for w, f in before:
@@ -459,11 +463,12 @@
 
     results = []
     make_terms(FAR, 1)
-    send_first(0)
-    send_first(1)
+    send_opposite(0)
     make_terms(RIGHT, 1)
     make_terms(LEFT, 1)
-    send_direct(0)
+    send_beside(0)
+    send_opposite(1)
+    send_beside(1)
     make_terms(OWN, 1)
     for copy in puts:
         copy.wait()
@@ -478,20 +483,17 @@
     for i, g in enumerate(gradients(0, span)):
         span_grad[i] = g[0:rows]
         other[i] = g[rows:span].astype(BF16)
-    send_second(0)
-    send_direct(1)
     pair = [
         go(remote(other.at[i], pair_in.at[i], pair_send.at[i], pair_recv.at[i], me.partner(mine))) for i in (0, 1)
     ]
     make_terms(FAR, 0)
-    send_first(2)
     make_terms(RIGHT, 0)
     make_terms(LEFT, 0)
-    send_second(1)
-    send_direct(2)
-    send_first(3)
+    for r in (2, 3, 4):
+        send_opposite(r)
+        send_beside(r)
+    make_terms(OWN, 0)
     send_ring(0)
-    make_terms(OWN, 0)
     for copy in mids:
         copy.wait()
     mids = [
@@ -506,11 +508,6 @@
     put = pltpu.make_async_copy(noisy_sum, ng, put_sem.at[0])
     put.start()
     for r in range(1, len(rounds)):
-        if r > 1:
-            send_direct(r + 1)
-            send_first(r + 2)
-        if r + 1 < len(rounds) or r == 1:
-            send_second(r + 1)
         if r == len(rounds) - 1:
             break
         send_ring(r)
@@ -583,7 +580,7 @@
             pltpu.VMEM((count, kw), BF16),
             pltpu.VMEM((stacked, count), F32),
             pltpu.VMEM((stacked, count), F32),
-            pltpu.VMEM((9, stacked, HEAD_SIZE), F32),
+            pltpu.VMEM((4, stacked, HEAD_SIZE), F32),
             pltpu.VMEM((stacked, HEAD_SIZE), F32),
             pltpu.VMEM((stacked, HEAD_SIZE), F32),
             pltpu.VMEM((stacked, HEAD_SIZE), F32),
@@ -591,10 +588,8 @@
             pltpu.VMEM((stacked, count), BF16),
             pltpu.VMEM((1, count), F32),
             pltpu.VMEM((NX, nz, 2, BLK, kw), BF16),
+            pltpu.VMEM((2, nz, 2, BLK, kw), BF16),
             pltpu.VMEM((nz, 2, BLK, kw), BF16),
-            pltpu.VMEM((nz, 2, 2 * BLK, kw), BF16),
-            pltpu.VMEM((nz, 2, BLK, kw), BF16),
-            pltpu.VMEM((nz, 2, 2 * BLK, kw), BF16),
             pltpu.VMEM((2, half + 1, 2, 2 * BLK, kw), BF16),
             pltpu.VMEM((2, half + 1, 2, 2 * BLK, kw), BF16),
             pltpu.VMEM((2, rows, kw), BF16),

time: 88.5 us -> 85.4 us (0.965)
  Pallas kernels: 87.4 us -> 84.4 us
    pallas_call x1, Pallas kernels: 85.5 us -> 82.5 us  [everything(): pl.pallas_call(functools.partial(kernel, nz, nh), out_shape=(shape(few, n...]
where the time goes in v4:
time: 85.4 us; the launch traced here: 85.2 us
  Pallas kernels  84.4 us (99%)
    pallas_call x1, Pallas kernels, everything(): pl.pallas_call(functools.partial(kernel, nz, nh), out_shape=(shape(few, n...  82.5 us
    pallas_call x1, Pallas kernels, settle(): pl.pallas_call(settle_kernel, out_shape=tuple((jax.ShapeDtypeStruct(*s) f...  1.91 us

profile of v4, /device:TPU:1, one launch (start us, length us, event | category | flops | bytes accessed | tf_op | source)
XLA Modules:
  0.0 85.2 jit_solution(15348896057507357347)
XLA Ops:
  0.6 82.5 %everything.1 = (bf16[24,6144]{1,0:T(8,128)(2,1)}, bf16[24,6144]{1,0:T(8,128)(2,1)}, bf16[24,1024]{1,0:T(8,128)(2,1)}, bf16[24,1024]{1,0:T(8,128)(2,1)}, bf16[8,...) custom-call(s32[64,64]{1,0:T(8,128)} %history.1, ...), custom_call_target="tpu_custom_call" | custom-call | tf_op jit(solution)/shard_map/everything/pallas_call | solution.py:553
  83.1 1.9 %settle.1 = (bf16[24,6144]{1,0:T(8,128)(2,1)}, bf16[24,6144]{1,0:T(8,128)(2,1)}, bf16[24,1024]{1,0:T(8,128)(2,1)}, bf16[24,1024]{1,0:T(8,128)(2,1)}, bf16[8,1024]{1,0:T(8,128)(2,1)}, /*index=5*/bf16[8,1024]{1,0:T(8,128)(2,1)}) custom-call(bf16[24,6144]{1,0:T(8,128)(2,1)} %get-tuple-element.12.refs_0_, bf16[24,6144]{1,0:T(8,128)(2,1)} %get-tuple-element.13.refs_1_, ...), custom_call_target="tpu_custom_call" | custom-call | tf_op jit(solution)/shard_map/settle/pallas_call | solution.py:629

commit v5 on v4

--- a/solution.py
+++ b/solution.py
@@ -406,9 +406,10 @@
                 remote(terms.at[FAR, p], far_in.at[p], x_send.at[2, p], x_recv.at[2, p], me.x_peer(2))
             )
 
-    def send_beside(r):
+    def send_beside(r, which=(0, 1)):
         for p in slots(r):
-            for i, (side, d) in enumerate(((RIGHT, 1), (LEFT, -1))):
+            for i in which:
+                side, d = ((RIGHT, 1), (LEFT, -1))[i]
                 beside[p, i] = go(
                     remote(terms.at[side, p], side_in.at[i, p], x_send.at[i, p], x_recv.at[i, p], me.x_peer(d))
                 )
@@ -465,8 +466,9 @@
     make_terms(FAR, 1)
     send_opposite(0)
     make_terms(RIGHT, 1)
+    send_beside(0, (0,))
     make_terms(LEFT, 1)
-    send_beside(0)
+    send_beside(0, (1,))
     send_opposite(1)
     send_beside(1)
     make_terms(OWN, 1)
@@ -511,7 +513,7 @@
         if r == len(rounds) - 1:
             break
         send_ring(r)
-        if r == 1:
+        if r == 2:
             put.wait()
             tail = [pltpu.make_async_copy(ng.at[i, token_rows(mine)], ref, own_sem.at[2 + i]) for i, ref in enumerate((own_k, own_v))]
             for copy in tail:

time: 85.4 us -> 85.5 us (level)
  no operation moved by 1% of the time
where the time goes in v5:
time: 85.5 us; the launch traced here: 85.2 us
  Pallas kernels  84.4 us (99%)
    pallas_call x1, Pallas kernels, everything(): pl.pallas_call(functools.partial(kernel, nz, nh), out_shape=(shape(few, n...  82.5 us
    pallas_call x1, Pallas kernels, settle(): pl.pallas_call(settle_kernel, out_shape=tuple((jax.ShapeDtypeStruct(*s) f...  1.91 us

profile of v5, /device:TPU:1, one launch (start us, length us, event | category | flops | bytes accessed | tf_op | source)
XLA Modules:
  0.0 85.2 jit_solution(13295257257996629629)
XLA Ops:
  0.6 82.5 %everything.1 = (bf16[24,6144]{1,0:T(8,128)(2,1)}, bf16[24,6144]{1,0:T(8,128)(2,1)}, bf16[24,1024]{1,0:T(8,128)(2,1)}, bf16[24,1024]{1,0:T(8,128)(2,1)}, bf16[8,...) custom-call(s32[64,64]{1,0:T(8,128)} %history.1, ...), custom_call_target="tpu_custom_call" | custom-call | tf_op jit(solution)/shard_map/everything/pallas_call | solution.py:555
  83.2 1.9 %settle.1 = (bf16[24,6144]{1,0:T(8,128)(2,1)}, bf16[24,6144]{1,0:T(8,128)(2,1)}, bf16[24,1024]{1,0:T(8,128)(2,1)}, bf16[24,1024]{1,0:T(8,128)(2,1)}, bf16[8,1024]{1,0:T(8,128)(2,1)}, /*index=5*/bf16[8,1024]{1,0:T(8,128)(2,1)}) custom-call(bf16[24,6144]{1,0:T(8,128)(2,1)} %get-tuple-element.12.refs_0_, bf16[24,6144]{1,0:T(8,128)(2,1)} %get-tuple-element.13.refs_1_, ...), custom_call_target="tpu_custom_call" | custom-call | tf_op jit(solution)/shard_map/settle/pallas_call | solution.py:631
